TPU v7x, 32 devices: a whole 2x2x4 slice. The times are simulated.
32 devices in a mesh: groups: 2 (over y), seq: 4 (over x, core), tensor: 4 (over z).
Axes of the slice: x: 2, y: 2, z: 4, core: 2. Of those that a mesh axis runs over, the one named last changes fastest.
Arguments:
- patches: bfloat16 [2056, 1280], P(('groups', 'seq')), parts along dimension 0, may hold values from -6 to 6
- latents: bfloat16 [64, 1280], replicated, may hold values from -160 to 160
- wq_res: bfloat16 [1280, 1536], P(None, 'tensor'), may hold values from -0.15625 to 0.15625
- wk_res: bfloat16 [1280, 1536], P(None, 'tensor'), may hold values from -0.3125 to 0.3125
- wv_res: bfloat16 [1280, 1536], P(None, 'tensor'), may hold values from -0.15625 to 0.15625
- wo_res: bfloat16 [1536, 1280], P('tensor'), may hold values from -0.625 to 0.625
- text: bfloat16 [3072, 8192], P('groups', 'seq'), parts along dimension 0, may hold values from -240 to 240
- norm_gain: bfloat16 [8192], P('seq'), may hold values from 0.25 to 1.75
- wq_x: bfloat16 [8192, 8192], P('seq', 'tensor'), may hold values from -0.0625 to 0.0625
- wk_x: bfloat16 [1280, 8192], P(None, 'tensor'), may hold values from -0.15625 to 0.15625
- wv_x: bfloat16 [1280, 8192], P(None, 'tensor'), may hold values from -0.15625 to 0.15625
- wo_x: bfloat16 [8192, 8192], P('tensor', 'seq'), may hold values from -0.25 to 0.25
- gate_x: float32 [8192], P('seq'), may hold values from -1.5 to 1.5
- text_image: int32 [3072], P('groups'), parts along dimension 0, may hold values from -1 to 3, as said below
Outputs:
- text_out: float32 [3072, 8192], P('groups', 'seq'), parts along dimension 0
- page_latents: bfloat16 [512, 1280], P(('groups', 'seq')), parts along dimension 0
There are 2 independent parts, one for each index of `groups`. A program takes and returns all parts, laid end to end along the dimension named above; an argument that names none is the same for every part. Nothing has to cross between parts.
Inputs may be any that keep to these rules, and one draw needn't show every extreme that they name: text_image[t] is the index of the last image placed at or before token t, -1 before the first image; it never falls along the tokens, and every one of the 4 images is the value of some tokens.
All inputs are finite; a program needn't handle non-finite values.
Results may differ from a plain program's by a relative error of at most 0.015.
The roundings to bfloat16 on the way count: a program that leaves them out, or rounds other values in their place, can miss the bound.
Values may be sent and summed in bfloat16 or wider, within the bound.
A program may use at most 192 MiB of HBM per device.

v0:
```python
import functools
import math

import jax
import jax.numpy as jnp
from jax import lax
from jax.experimental import pallas as pl
from jax.experimental.pallas import tpu as pltpu
from jax.sharding import PartitionSpec as P

HEAD = 128
RES_HEAD = 96
PATCH_IMG = 257
SUB = 32
LEAD = 9
SUM_STEP, PAGE_STEP, PASS_STEP = 3, 6, 8
EARLY, LATER = 3, 7
RING = 4
BF = jnp.bfloat16
F32 = jnp.float32


def resample(patches, latents, wq_res, wk_res, wv_res, wo_res):
    inv_res = 1.0 / math.sqrt(RES_HEAD)
    lat_count = latents.shape[0]
    img_count = patches.shape[0] // PATCH_IMG
    heads_res = wq_res.shape[1] // RES_HEAD
    queries = (
        jnp.dot(latents, wq_res, preferred_element_type=F32)
        .astype(BF)
        .reshape(lat_count, heads_res, RES_HEAD)
    )
    page_keys = (
        jnp.dot(patches, wk_res, preferred_element_type=F32)
        .astype(BF)
        .reshape(img_count, PATCH_IMG, heads_res, RES_HEAD)
    )
    page_values = (
        jnp.dot(patches, wv_res, preferred_element_type=F32)
        .astype(BF)
        .reshape(img_count, PATCH_IMG, heads_res, RES_HEAD)
    )
    scores = jnp.einsum("lhd,iphd->ihlp", queries, page_keys, preferred_element_type=F32) * inv_res
    summit = jnp.max(scores, axis=3, keepdims=True)
    weights = jnp.exp(scores - summit).astype(BF)
    totals = jnp.sum(weights, axis=3, dtype=F32)
    blended = jnp.einsum("ihlp,iphd->ihld", weights, page_values, preferred_element_type=F32)
    pooled = (
        (blended / totals[:, :, :, None])
        .transpose(0, 2, 1, 3)
        .reshape(img_count * lat_count, heads_res * RES_HEAD)
        .astype(BF)
    )
    return jnp.dot(pooled, wo_res, preferred_element_type=F32)


def flow_kernel(dims, *refs):
    n_x, n, count, sub, owners, shared = dims
    (part_ref, lat_ref, gain_ref, img_ref, own_ref, text_ref, wq_ref, wk_ref, wv_ref, wo_ref) = refs[:10]
    out_ref, page_ref = refs[10:12]
    (wq, wkv, late, text, own_half, away_out, away_in, x_out, x_in, sq_half, sq_away_out, sq_away_in,
     sq_x_out, sq_x_in, query, keys, values, pages, lat_in, att, part, came) = refs[12:34]
    (load_sem, text_sem, qc_send, qc_recv, qx_send, qx_recv, lat_send, lat_recv, pz_send, pz_recv,
     pg_send, pg_x, pg_core, side_sem, core_sem, block_sem, in_sem, back_sem, inward_sem,
     outward_sem) = refs[34:]
    n_seq, half = 2 * n_x, n // 2
    total = count * n_seq
    rows_all, rows_half = n_seq * sub, n_x * sub
    seq_me, me = lax.axis_index("seq"), lax.axis_index("tensor")
    core, x_me = seq_me % 2, seq_me // 2
    partner = 2 * x_me + 1 - core
    own = core * n_x + x_me
    side = me // half
    depth = me * (1 - side) + (n - 1 - me) * side
    inner, outer = me + 1 - 2 * side, me - 1 + 2 * side
    lag = 2 + 4 * (half - 1 - depth)
    feat, qwidth = wq.shape
    width = wo_ref.shape[1]
    heads = qwidth // HEAD
    scale = 1.0 / math.sqrt(HEAD)
    lat_rows = part_ref.shape[0]
    vis = part_ref.shape[1]
    part_rows = lat_rows // owners
    stride = n // owners
    wo = wkv if shared else late

    def remote(src, dst, sent, got, **where):
        return pltpu.make_async_remote_copy(
            src_ref=src, dst_ref=dst, send_sem=sent, recv_sem=got,
            device_id=where, device_id_type=pl.DeviceIdType.MESH,
        )

    def other_x(j):
        return (x_me + j) % n_x

    def other_z(j):
        return (me + j) % n

    def load_text(c):
        rows = pl.ds(pl.multiple_of(c * rows_all, rows_all), rows_all)
        return pltpu.make_async_copy(text_ref.at[rows], text.at[c % RING], text_sem.at[c % RING])

    load_q = pltpu.make_async_copy(wq_ref, wq, load_sem.at[0])
    load_k = pltpu.make_async_copy(wk_ref, wkv.at[pl.ds(0, vis)], load_sem.at[1])
    load_v = pltpu.make_async_copy(wv_ref, wkv.at[pl.ds(vis, vis)], load_sem.at[2])
    load_o = pltpu.make_async_copy(wo_ref, wo.at[pl.ds(0, qwidth)], load_sem.at[3])

    def lat_piece(j):
        rows = pl.ds(j * part_rows, part_rows)
        return remote(
            part_ref.at[rows], lat_in.at[me], lat_send.at[j], lat_recv.at[me], tensor=j * stride
        )

    def page_rows(j):
        return pl.ds(pl.multiple_of(j * part_rows, part_rows), part_rows)

    def page_piece(j, z, k):
        ref = pages.at[seq_me, page_rows(j)]
        return remote(ref, ref, pz_send.at[k], pz_recv.at[j], tensor=z)

    def page_core(x, j):
        ref = pages.at[2 * x + core]
        return remote(ref, ref, pg_send.at[j], pg_core.at[x], seq=partner)

    def page_from_core(x):
        ref = pages.at[2 * x + 1 - core]
        return remote(ref, ref, pg_send.at[0], pg_core.at[x], seq=partner)

    def page_x(j):
        ref = pages.at[seq_me]
        return remote(
            ref, ref, pg_send.at[n_x + j - 1], pg_x.at[x_me], seq=2 * other_x(j) + core
        )

    def page_from_x(j):
        x = other_x(j)
        ref = pages.at[2 * x + core]
        return remote(ref, ref, pg_send.at[n_x + j - 1], pg_x.at[x], seq=2 * x + core)

    def away(c, which):
        src, dst = (away_out, away_in) if which == 0 else (sq_away_out, sq_away_in)
        return remote(
            src.at[c % RING], dst.at[c], qc_send.at[which, c % RING], qc_recv.at[which, c], seq=partner
        )

    def aside(c, j, which):
        src, dst = (x_out, x_in) if which == 0 else (sq_x_out, sq_x_in)
        return remote(
            src.at[c % RING, j - 1], dst.at[c, j - 1], qx_send.at[which, c % RING, j - 1],
            qx_recv.at[which, c, j - 1], seq=2 * other_x(j) + core,
        )

    def to_core(c, x, j):
        ref = att.at[c, core * n_x + x]
        return remote(ref, ref, block_sem.at[c, j], core_sem.at[c, x], seq=partner)

    def from_core(c, x):
        ref = att.at[c, (1 - core) * n_x + x]
        return remote(ref, ref, block_sem.at[c, 0], core_sem.at[c, x], seq=partner)

    def to_x(c, j):
        ref = att.at[c, own]
        return remote(
            ref, ref, block_sem.at[c, n_x + j - 1], side_sem.at[c, x_me], seq=2 * other_x(j) + core
        )

    def from_x(c, j):
        x = other_x(j)
        ref = att.at[c, core * n_x + x]
        return remote(ref, ref, block_sem.at[c, n_x + j - 1], side_sem.at[c, x], seq=2 * x + core)

    def rows_of(p):
        return pl.ds(pl.multiple_of(p * sub, sub), sub)

    def inward(p):
        return remote(part.at[p], came.at[p], inward_sem.at[p], in_sem.at[p], tensor=inner)

    def across(p):
        return remote(
            part.at[p], out_ref.at[rows_of(p)], inward_sem.at[p], back_sem.at[p], tensor=inner
        )

    def outward(p):
        ref = out_ref.at[rows_of(p)]
        return remote(ref, ref, outward_sem.at[p], back_sem.at[p], tensor=outer)

    def half_rows(which):
        return pl.ds(pl.multiple_of(which * rows_half, rows_half), rows_half)

    def strip(x):
        return pl.ds(pl.multiple_of(x * sub, sub), sub)

    def project(c):
        slot = c % RING
        load_text(c).wait()

        @pl.when(c >= RING)
        def _():
            for which in (0, 1):
                away(c - RING, which).wait_send()

        rows = jnp.concatenate(
            [text[slot, half_rows(1 - core)], text[slot, half_rows(core)]], axis=0
        ).astype(F32)
        squares = rows * rows
        sums = squares[:, :128]
        for g in range(1, feat // 128):
            sums = sums + squares[:, g * 128 : (g + 1) * 128]
        sq_away_out[slot] = sums[:rows_half]
        sq_half[c] = sums[rows_half:]
        scaled = (rows * gain_ref[...].astype(F32)).astype(BF)
        tile = math.gcd(qwidth, 1024)
        for t in range(0, qwidth, tile):
            value = jnp.dot(scaled, wq[:, t : t + tile], preferred_element_type=F32)
            away_out[slot, :, t : t + tile] = value[:rows_half].astype(BF)
            own_half[c, :, t : t + tile] = value[rows_half:]
        for which in (0, 1):
            away(c, which).start()

        @pl.when(c + RING < count)
        def _():
            load_text(c + RING).start()

    def scatter(c):
        slot = c % RING
        for which in (0, 1):
            away(c, which).wait_recv()

        @pl.when(c >= RING)
        def _():
            for j in range(1, n_x):
                for which in (0, 1):
                    aside(c - RING, j, which).wait_send()

        for j in range(1, n_x):
            rows = strip(other_x(j))
            x_out[slot, j - 1] = (own_half[c, rows] + away_in[c, rows].astype(F32)).astype(BF)
            sq_x_out[slot, j - 1] = sq_half[c, rows] + sq_away_in[c, rows]
            for which in (0, 1):
                aside(c, j, which).start()

    def finish(c):
        rows = strip(x_me)
        value = own_half[c, rows] + away_in[c, rows].astype(F32)
        square = sq_half[c, rows] + sq_away_in[c, rows]
        for j in range(1, n_x):
            for which in (0, 1):
                aside(c, j, which).wait_recv()
            value = value + x_in[c, j - 1].astype(F32)
            square = square + sq_x_in[c, j - 1]
        mean = jnp.sum(square, axis=1, keepdims=True) / (feat * n_seq)
        query[...] = (value * lax.rsqrt(mean + 1e-05)).astype(BF)

    def attend(c):
        img = img_ref[strip(c)]
        allowed = img == own_ref[...]
        visible = (img >= 0).astype(F32)
        cuts = [slice(h * HEAD, (h + 1) * HEAD) for h in range(heads)]
        logits = [
            lax.dot_general(
                query[:, cut], keys[:, cut], (((1,), (1,)), ((), ())), preferred_element_type=F32
            )
            for cut in cuts
        ]
        logits = [jnp.where(allowed, value * scale, -1e30) for value in logits]
        peaks = [jnp.max(value, axis=1, keepdims=True) for value in logits]
        probs = [jnp.exp(value - peak).astype(BF) for value, peak in zip(logits, peaks)]
        weights = [jnp.sum(p.astype(F32), axis=1, keepdims=True) for p in probs]
        mixed = [
            jnp.dot(p, values[:, cut], preferred_element_type=F32) for p, cut in zip(probs, cuts)
        ]
        for value, weight, cut in zip(mixed, weights, cuts):
            att[c, own, :, cut] = (value / weight * visible).astype(BF)
        for j in range(1, n_x):
            to_x(c, j).start()
        to_core(c, x_me, 0).start()

    def product(c):
        tile = math.gcd(width, 1024)

        @pl.loop(0, width // tile)
        def _(t):
            cols = pl.ds(pl.multiple_of(t * tile, tile), tile)
            rows = att[c].reshape(rows_all, qwidth)
            value = jnp.dot(rows, wo[:qwidth, cols], preferred_element_type=F32).astype(BF)
            for b in range(n_seq):
                part[c * n_seq + b, :, cols] = value[b * sub : (b + 1) * sub]

    def gather(p):
        @pl.when(depth > 0)
        def _():
            inward(p).wait_recv()
            part[p] = (part[p].astype(F32) + came[p].astype(F32)).astype(BF)

        @pl.when(depth < half - 1)
        def _():
            inward(p).start()

        @pl.when(depth == half - 1)
        def _():
            across(p).start()

    def spread(p):
        outward(p).wait_recv()

        @pl.when(depth == half - 1)
        def _():
            rows = rows_of(p)
            out_ref[rows] = (part[p].astype(F32) + out_ref[rows].astype(F32)).astype(BF)

        @pl.when(depth > 0)
        def _():
            outward(p).start()

    def sum_latents():
        @pl.when(me % stride == 0)
        def _():
            j = me // stride
            rows = page_rows(j)
            value = part_ref[rows]
            for k in range(1, n):
                z = other_z(k)
                remote(
                    part_ref.at[rows], lat_in.at[z], lat_send.at[0], lat_recv.at[z], tensor=z
                ).wait_recv()
                value = value + lat_in[z]
            base = (j * part_rows) % lat_ref.shape[0]
            mine = lat_ref[pl.ds(pl.multiple_of(base, part_rows), part_rows)].astype(F32)
            pages[seq_me, rows] = (mine + value).astype(BF)
            for k in range(1, n):
                page_piece(j, other_z(k), k - 1).start()

    def share_page():
        for j in range(owners):
            @pl.when(me != j * stride)
            def _(j=j):
                page_piece(j, j * stride, 0).wait_recv()

        for j in range(1, n_x):
            page_x(j).start()
        page_core(x_me, 0).start()
        page_ref[...] = pages[seq_me]

    def pass_pages():
        for j in range(1, n_x):
            page_from_x(j).wait_recv()
            page_core(other_x(j), j).start()

    def keys_values():
        load_k.wait()
        load_v.wait()
        for x in range(n_x):
            page_from_core(x).wait_recv()
        rows = pages[...].reshape(n_seq * lat_rows, vis)
        tile = math.gcd(qwidth, 1024)
        for base, target in ((0, keys), (vis, values)):
            @pl.loop(0, qwidth // tile)
            def _(t, base=base, target=target):
                cols = pl.ds(pl.multiple_of(t * tile, tile), tile)
                target[:, cols] = jnp.dot(
                    rows, wkv[base : base + vis, cols], preferred_element_type=F32
                ).astype(BF)
        if shared:
            load_o.start()

    load_text(0).start()
    load_q.start()
    for c in range(1, min(RING, count)):
        load_text(c).start()
    load_k.start()
    load_v.start()
    if not shared:
        load_o.start()

    barrier = pltpu.get_barrier_semaphore()

    def greet(**where):
        pl.semaphore_signal(barrier, inc=1, device_id=where, device_id_type=pl.DeviceIdType.MESH)

    greet(seq=partner)
    for j in range(1, n_x):
        greet(seq=2 * other_x(j) + core)
    for j in range(1, n):
        greet(tensor=other_z(j))
    pl.semaphore_wait(barrier, 1 + (n_x - 1) + (n - 1))

    for j in range(owners):
        @pl.when(me != j * stride)
        def _(j=j):
            lat_piece(j).start()

    load_q.wait()

    @pl.loop(0, count + LEAD + 1)
    def _(s):
        pl.when(s == SUM_STEP)(sum_latents)
        pl.when(s == PAGE_STEP)(share_page)
        pl.when(s == PASS_STEP)(pass_pages)

        @pl.when(s < count)
        def _():
            project(s)

        later = jnp.maximum(s - LATER, 0)

        @pl.when(jnp.logical_or(s == EARLY, jnp.logical_and(later >= 1, later < count)))
        def _():
            scatter(later)

        c = s - LEAD - 1

        @pl.when(c >= 0)
        def _():
            for j in range(1, n_x):
                from_x(c, j).wait_recv()
                to_core(c, other_x(j), j).start()

        pl.when(s == LEAD)(keys_values)

        @pl.when(jnp.logical_and(s >= LEAD, s < LEAD + count))
        def _():
            finish(s - LEAD)
            attend(s - LEAD)

        pl.when(c == 0)(load_o.wait)

        @pl.when(c >= 0)
        def _():
            for x in range(n_x):
                from_core(c, x).wait_recv()
            product(c)

            @pl.loop(0, n_seq)
            def _(b):
                p = c * n_seq + b
                gather(p)

                @pl.when(jnp.logical_and(depth > 0, p >= lag))
                def _():
                    spread(p - lag)

    @pl.loop(0, total)
    def _(p):
        @pl.when(jnp.logical_or(depth == 0, p >= total - lag))
        def _():
            spread(p)

    @pl.loop(0, total)
    def _(p):
        inward(p).wait_send()

        @pl.when(depth > 0)
        def _():
            outward(p).wait_send()

    @pl.loop(0, count)
    def _(c):
        for j in range(n_x):
            to_core(c, x_me, j).wait_send()
        for j in range(1, n_x):
            to_x(c, j).wait_send()

    for c in range(max(count - RING, 0), count):
        for which in (0, 1):
            away(c, which).wait_send()
            for j in range(1, n_x):
                aside(c, j, which).wait_send()
    for j in range(n_x):
        page_core(x_me, j).wait_send()
    for j in range(1, n_x):
        page_x(j).wait_send()
    for j in range(owners):
        @pl.when(me != j * stride)
        def _(j=j):
            lat_piece(j).wait_send()

    @pl.when(me % stride == 0)
    def _():
        for k in range(1, n):
            page_piece(me // stride, other_z(k), k - 1).wait_send()


def flow(partial_value, latents, gain, img, owner, text, wq, wk, wv, wo, n_x, n):
    n_seq = 2 * n_x
    tokens, feat = text.shape
    qwidth, width = wo.shape
    lat_rows, vis = partial_value.shape
    sub = math.gcd(tokens // n_seq, SUB)
    count = tokens // (n_seq * sub)
    pieces = count * n_seq
    owners = math.gcd(n, lat_rows // 16)
    shared = qwidth == width and qwidth <= 2 * vis
    dma = pltpu.SemaphoreType.DMA
    vmem, anywhere = pl.BlockSpec(memory_space=pltpu.VMEM), pl.BlockSpec(memory_space=pl.ANY)
    others = max(n_x - 1, 1)
    half_rows = n_x * sub
    scratch = [
        ((feat, qwidth), BF),
        ((2 * vis, qwidth), BF),
        ((16, 128) if shared else (qwidth, width), BF),
        ((RING, n_seq * sub, feat), BF),
        ((count, half_rows, qwidth), F32),
        ((RING, half_rows, qwidth), BF),
        ((count, half_rows, qwidth), BF),
        ((RING, others, sub, qwidth), BF),
        ((count, others, sub, qwidth), BF),
        ((count, half_rows, 128), F32),
        ((RING, half_rows, 128), F32),
        ((count, half_rows, 128), F32),
        ((RING, others, sub, 128), F32),
        ((count, others, sub, 128), F32),
        ((sub, qwidth), BF),
        ((n_seq * lat_rows, qwidth), BF),
        ((n_seq * lat_rows, qwidth), BF),
        ((n_seq, lat_rows, vis), BF),
        ((n, lat_rows // owners, vis), F32),
        ((count, n_seq, sub, qwidth), BF),
        ((pieces, sub, width), BF),
        ((pieces, sub, width), BF),
    ]
    return pl.pallas_call(
        functools.partial(flow_kernel, (n_x, n, count, sub, owners, shared)),
        out_shape=(
            jax.ShapeDtypeStruct((tokens, width), BF),
            jax.ShapeDtypeStruct((lat_rows, vis), BF),
        ),
        in_specs=[vmem] * 5 + [anywhere] * 5,
        out_specs=(vmem, vmem),
        scratch_shapes=[pltpu.VMEM(shape, kind) for shape, kind in scratch]
        + [
            dma((4,)),
            dma((RING,)),
            dma((2, RING)),
            dma((2, count)),
            dma((2, RING, others)),
            dma((2, count, others)),
            dma((owners,)),
            dma((n,)),
            dma((n,)),
            dma((owners,)),
            dma((2 * n_x,)),
            dma((n_x,)),
            dma((n_x,)),
            dma((count, n_x)),
            dma((count, n_x)),
            dma((count, 2 * n_x - 1)),
        ]
        + [dma((pieces,))] * 4,
        compiler_params=pltpu.CompilerParams(
            collective_id=0, has_side_effects=True, vmem_limit_bytes=63 << 20
        ),
        name="flow",
    )(partial_value, latents, gain, img, owner, text, wq, wk, wv, wo)


def close_kernel(rows, text_ref, gate_ref, branch_ref, out_ref):
    at = pl.multiple_of(pl.program_id(0) * rows, rows)
    branch = branch_ref[pl.ds(at, rows)].astype(F32)
    out_ref[...] = text_ref[...].astype(F32) + jnp.tanh(gate_ref[...]) * branch


def close(text, gate, branch):
    tokens, width = text.shape
    rows = math.gcd(tokens, 128)
    block = pl.BlockSpec((rows, width), lambda i: (i, 0))
    whole = pl.BlockSpec(memory_space=pltpu.VMEM)
    return pl.pallas_call(
        functools.partial(close_kernel, rows),
        out_shape=jax.ShapeDtypeStruct((tokens, width), F32),
        grid=(tokens // rows,),
        in_specs=[block, whole, whole],
        out_specs=block,
        compiler_params=pltpu.CompilerParams(vmem_limit_bytes=16 << 20),
        name="close",
    )(text, gate, branch)


def make_shards(n_seq, n_tensor):
    n_x = n_seq // 2

    def shards(
        patches,
        latents,
        wq_res,
        wk_res,
        wv_res,
        wo_res,
        text,
        norm_gain,
        wq_x,
        wk_x,
        wv_x,
        wo_x,
        gate_x,
        text_image,
    ):
        seq_me = lax.axis_index("seq")
        block = (seq_me % 2) * n_x + seq_me // 2
        lat_count = latents.shape[0]
        tokens = text.shape[0]
        sub = math.gcd(tokens // n_seq, SUB)
        img = lax.dynamic_index_in_dim(
            text_image.reshape(-1, n_seq, sub), block, 1, keepdims=False
        ).reshape(-1, 1)
        partial_value = resample(patches, latents, wq_res, wk_res, wv_res, wo_res)
        owner = jnp.arange(n_seq * partial_value.shape[0], dtype=jnp.int32) // lat_count
        branch, page_latents = flow(
            partial_value, latents, norm_gain[None, :], img, owner[None, :], text,
            wq_x, wk_x, wv_x, wo_x, n_x, n_tensor,
        )
        return close(text, gate_x[None, :], branch), page_latents

    return shards


def solution(mesh):
    in_specs = (
        P(("groups", "seq"), None),
        P(),
        P(None, "tensor"),
        P(None, "tensor"),
        P(None, "tensor"),
        P("tensor", None),
        P("groups", "seq"),
        P("seq"),
        P("seq", "tensor"),
        P(None, "tensor"),
        P(None, "tensor"),
        P("tensor", "seq"),
        P("seq"),
        P("groups"),
    )
    out_specs = (P("groups", "seq"), P(("groups", "seq"), None))
    body = make_shards(mesh.shape["seq"], mesh.shape["tensor"])
    return jax.shard_map(body, mesh=mesh, in_specs=in_specs, out_specs=out_specs, check_vma=False)
```

profile of v0, /device:TPU:0, one launch (start us, length us, event | category | flops | bytes accessed | tf_op | source)
XLA Modules:
  0.0 219.7 jit_solution(10252165136138700873)
XLA Ops:
  0.6 0.0 copy-start
  0.6 0.0 copy-start.4
  0.7 0.6 and_select_fusion.refs_4_
  1.3 1.3 broadcast_in_dim.10.refs_2_
  2.6 0.8 reshape.83
  3.4 1.6 convolution_convert_fusion.2
  5.0 0.1 reshape.80
  5.1 0.9 reshape.85.refs_3_
  5.9 0.0 copy-done
  5.9 1.6 convolution_convert_fusion.1
  7.5 0.3 reshape.79
  7.9 0.3 fusion.7
  8.2 0.2 convert_reduce_fusion
  8.4 1.9 convolution_convert_fusion
  10.4 0.3 reshape.82
  10.7 0.3 fusion.2
  11.0 0.1 copy.22
  11.0 0.1 convert_element_type.35
  11.1 0.0 copy-done.4
  11.1 1.0 fusion.8.refs_0_
  12.2 193.6 %flow.1 = (bf16[1536,2048]{1,0:T(8,128)(2,1)}, bf16[64,1280]{1,0:T(8,128)(2,1)}) custom-call(f32[64,1280]{1,0:T(8,128)} %fusion.8.refs_0_, bf16[64,1280]{1,0:T(8,128)(2,1)} %refs_1_.1, bf16[1,2048]{1,0:T(2,128)(2,1)} %broadcast_in_dim.10.refs_2_, s32[384,1]{1,0:T(8,128)} %reshape.85.refs_3_, s32[1,256]{1,0:T(1,128)} %and_select_fusion.refs_4_, ...), custom_call_target="tpu_custom_call" | custom-call | tf_op jit(solution)/shard_map/flow/pallas_call | solution.py:521
  205.8 0.0 copy-start.1
  205.8 2.8 %copy-done.1 = bf16[1536,2048]{1,0:T(8,128)(2,1)S(1)} copy-done((bf16[1536,2048]{1,0:T(8,128)(2,1)S(1)}, bf16[1536,2048]{1,0:T(8,128)(2,1)}, u32[]{:S(2)}) %copy-start.1) | copy-done | bytes 6291480
  208.6 0.0 copy-start.2
  208.6 2.8 %copy-done.2 = bf16[1536,2048]{1,0:T(8,128)(2,1)S(1)} copy-done((bf16[1536,2048]{1,0:T(8,128)(2,1)S(1)}, bf16[1536,2048]{1,0:T(8,128)(2,1)}, u32[]{:S(2)}) %copy-start.2) | copy-done | bytes 6291480
  211.4 0.0 copy-start.3
  211.4 0.7 copy-done.3
  212.1 0.0 copy-start.5
  212.1 7.0 %close.1 = f32[1536,2048]{1,0:T(8,128)} custom-call(bf16[1536,2048]{1,0:T(8,128)(2,1)S(1)} %copy-done.1, f32[1,2048]{1,0:T(1,128)S(1)} %bitcast.20, bf16[1536,2048]{1,0:T(8,128)(2,1)S(1)} %copy-done.2), custom_call_target="tpu_custom_call" | custom-call | tf_op jit(solution)/shard_map/close/pallas_call | solution.py:567
  219.1 0.0 copy-done.5
  219.1 0.7 copy.35
  (1 shorter events, 0.0 us)
Async XLA Ops:
  0.6 5.3 %copy-start = (bf16[1280,384]{1,0:T(8,128)(2,1)S(1)}, bf16[1280,384]{1,0:T(8,128)(2,1)}, u32[]{:S(2)}) copy-start(bf16[1280,384]{1,0:T(8,128)(2,1)} %param.17) | copy-start | bytes 2949124
  0.6 10.5 %copy-start.4 = (bf16[384,1280]{1,0:T(8,128)(2,1)S(1)}, bf16[384,1280]{1,0:T(8,128)(2,1)}, u32[]{:S(2)}) copy-start(bf16[384,1280]{1,0:T(8,128)(2,1)} %param.19) | copy-start | bytes 2949124
  205.8 2.8 %copy-start.1 = (bf16[1536,2048]{1,0:T(8,128)(2,1)S(1)}, bf16[1536,2048]{1,0:T(8,128)(2,1)}, u32[]{:S(2)}) copy-start(bf16[1536,2048]{1,0:T(8,128)(2,1)} %text_ref.1) | copy-start | bytes 18874372
  208.6 2.8 %copy-start.2 = (bf16[1536,2048]{1,0:T(8,128)(2,1)S(1)}, bf16[1536,2048]{1,0:T(8,128)(2,1)}, u32[]{:S(2)}) copy-start(bf16[1536,2048]{1,0:T(8,128)(2,1)} %get-tuple-element.4.branch_ref) | copy-start | bytes 18874372
  211.4 0.7 copy-start.3
  212.1 7.0 %copy-start.5 = (bf16[64,1280]{1,0:T(8,128)(2,1)S(1)}, bf16[64,1280]{1,0:T(8,128)(2,1)}, u32[]{:S(2)}) copy-start(bf16[64,1280]{1,0:T(8,128)(2,1)} %get-tuple-element.11) | copy-start | bytes 491524
where the time goes:
time: 220 us
  Pallas kernels  201 us (91%)
  local copies, waits for them, and re-layouts  10.8 us (5%)
  matrix products  6.69 us (3%)
    pallas_call x1, Pallas kernels, flow(): pl.pallas_call(functools.partial(flow_kernel, (n_x, n, count, sub, owners...  194 us
    pallas_call x1, Pallas kernels, close(): pl.pallas_call(functools.partial(close_kernel, rows), out_shape=jax.Shape...  7.02 us
    unnamed x13, local copies, waits for them, and re-layouts  6.94 us

commit v1 on v0

--- a/solution.py
+++ b/solution.py
@@ -15,7 +15,7 @@
 LEAD = 9
 SUM_STEP, PAGE_STEP, PASS_STEP = 3, 6, 8
 EARLY, LATER = 3, 7
-RING = 4
+RING = 2
 BF = jnp.bfloat16
 F32 = jnp.float32
 
@@ -55,16 +55,17 @@
 
 
 def flow_kernel(dims, *refs):
-    n_x, n, count, sub, owners, shared = dims
+    n_x, n, count, sub, owners, shared, first = dims
     (part_ref, lat_ref, gain_ref, img_ref, own_ref, text_ref, wq_ref, wk_ref, wv_ref, wo_ref) = refs[:10]
-    out_ref, page_ref = refs[10:12]
-    (wq, wkv, late, text, own_half, away_out, away_in, x_out, x_in, sq_half, sq_away_out, sq_away_in,
-     sq_x_out, sq_x_in, query, keys, values, pages, lat_in, att, part, came) = refs[12:34]
+    out_ref, text, page_ref = refs[10:13]
+    (wq, wkv, late, own_half, away_out, away_in, x_out, x_in, sq_half, sq_away_out, sq_away_in,
+     sq_x_out, sq_x_in, query, keys, values, pages, lat_in, att, second, came, mixed_rows) = refs[13:35]
     (load_sem, text_sem, qc_send, qc_recv, qx_send, qx_recv, lat_send, lat_recv, pz_send, pz_recv,
      pg_send, pg_x, pg_core, side_sem, core_sem, block_sem, in_sem, back_sem, inward_sem,
-     outward_sem) = refs[34:]
+     outward_sem, free_sem) = refs[35:]
     n_seq, half = 2 * n_x, n // 2
     total = count * n_seq
+    keep = own_half.shape[0]
     rows_all, rows_half = n_seq * sub, n_x * sub
     seq_me, me = lax.axis_index("seq"), lax.axis_index("tensor")
     core, x_me = seq_me % 2, seq_me // 2
@@ -83,6 +84,7 @@
     part_rows = lat_rows // owners
     stride = n // owners
     wo = wkv if shared else late
+    part = att if shared else second
 
     def remote(src, dst, sent, got, **where):
         return pltpu.make_async_remote_copy(
@@ -98,7 +100,7 @@
 
     def load_text(c):
         rows = pl.ds(pl.multiple_of(c * rows_all, rows_all), rows_all)
-        return pltpu.make_async_copy(text_ref.at[rows], text.at[c % RING], text_sem.at[c % RING])
+        return pltpu.make_async_copy(text_ref.at[rows], text.at[rows], text_sem.at[c])
 
     load_q = pltpu.make_async_copy(wq_ref, wq, load_sem.at[0])
     load_k = pltpu.make_async_copy(wk_ref, wkv.at[pl.ds(0, vis)], load_sem.at[1])
@@ -118,24 +120,24 @@
         ref = pages.at[seq_me, page_rows(j)]
         return remote(ref, ref, pz_send.at[k], pz_recv.at[j], tensor=z)
 
-    def page_core(x, j):
-        ref = pages.at[2 * x + core]
-        return remote(ref, ref, pg_send.at[j], pg_core.at[x], seq=partner)
-
-    def page_from_core(x):
-        ref = pages.at[2 * x + 1 - core]
-        return remote(ref, ref, pg_send.at[0], pg_core.at[x], seq=partner)
-
-    def page_x(j):
-        ref = pages.at[seq_me]
+    def page_core(x, j, k):
+        ref = pages.at[2 * x + core, page_rows(k)]
+        return remote(ref, ref, pg_send.at[j, k], pg_core.at[x, k], seq=partner)
+
+    def page_from_core(x, k):
+        ref = pages.at[2 * x + 1 - core, page_rows(k)]
+        return remote(ref, ref, pg_send.at[0, k], pg_core.at[x, k], seq=partner)
+
+    def page_x(j, k):
+        ref = pages.at[seq_me, page_rows(k)]
         return remote(
-            ref, ref, pg_send.at[n_x + j - 1], pg_x.at[x_me], seq=2 * other_x(j) + core
-        )
-
-    def page_from_x(j):
+            ref, ref, pg_send.at[n_x + j - 1, k], pg_x.at[x_me, k], seq=2 * other_x(j) + core
+        )
+
+    def page_from_x(j, k):
         x = other_x(j)
-        ref = pages.at[2 * x + core]
-        return remote(ref, ref, pg_send.at[n_x + j - 1], pg_x.at[x], seq=2 * x + core)
+        ref = pages.at[2 * x + core, page_rows(k)]
+        return remote(ref, ref, pg_send.at[n_x + j - 1, k], pg_x.at[x, k], seq=2 * x + core)
 
     def away(c, which):
         src, dst = (away_out, away_in) if which == 0 else (sq_away_out, sq_away_in)
@@ -151,29 +153,34 @@
         )
 
     def to_core(c, x, j):
-        ref = att.at[c, core * n_x + x]
+        ref = att.at[c * n_seq + core * n_x + x]
         return remote(ref, ref, block_sem.at[c, j], core_sem.at[c, x], seq=partner)
 
     def from_core(c, x):
-        ref = att.at[c, (1 - core) * n_x + x]
+        ref = att.at[c * n_seq + (1 - core) * n_x + x]
         return remote(ref, ref, block_sem.at[c, 0], core_sem.at[c, x], seq=partner)
 
     def to_x(c, j):
-        ref = att.at[c, own]
+        ref = att.at[c * n_seq + own]
         return remote(
             ref, ref, block_sem.at[c, n_x + j - 1], side_sem.at[c, x_me], seq=2 * other_x(j) + core
         )
 
     def from_x(c, j):
         x = other_x(j)
-        ref = att.at[c, core * n_x + x]
+        ref = att.at[c * n_seq + core * n_x + x]
         return remote(ref, ref, block_sem.at[c, n_x + j - 1], side_sem.at[c, x], seq=2 * x + core)
 
     def rows_of(p):
         return pl.ds(pl.multiple_of(p * sub, sub), sub)
 
-    def inward(p):
-        return remote(part.at[p], came.at[p], inward_sem.at[p], in_sem.at[p], tensor=inner)
+    def landing(p, early):
+        if early:
+            return came.at[p]
+        return wq.at[pl.ds(pl.multiple_of((p - first) * sub, sub), sub)]
+
+    def inward(p, early):
+        return remote(part.at[p], landing(p, early), inward_sem.at[p], in_sem.at[p], tensor=inner)
 
     def across(p):
         return remote(
@@ -200,7 +207,7 @@
                 away(c - RING, which).wait_send()
 
         rows = jnp.concatenate(
-            [text[slot, half_rows(1 - core)], text[slot, half_rows(core)]], axis=0
+            [text[half_rows(2 * c + 1 - core)], text[half_rows(2 * c + core)]], axis=0
         ).astype(F32)
         squares = rows * rows
         sums = squares[:, :128]
@@ -213,13 +220,9 @@
         for t in range(0, qwidth, tile):
             value = jnp.dot(scaled, wq[:, t : t + tile], preferred_element_type=F32)
             away_out[slot, :, t : t + tile] = value[:rows_half].astype(BF)
-            own_half[c, :, t : t + tile] = value[rows_half:]
+            own_half[c % keep, :, t : t + tile] = value[rows_half:]
         for which in (0, 1):
             away(c, which).start()
-
-        @pl.when(c + RING < count)
-        def _():
-            load_text(c + RING).start()
 
     def scatter(c):
         slot = c % RING
@@ -234,14 +237,14 @@
 
         for j in range(1, n_x):
             rows = strip(other_x(j))
-            x_out[slot, j - 1] = (own_half[c, rows] + away_in[c, rows].astype(F32)).astype(BF)
+            x_out[slot, j - 1] = (own_half[c % keep, rows] + away_in[c, rows].astype(F32)).astype(BF)
             sq_x_out[slot, j - 1] = sq_half[c, rows] + sq_away_in[c, rows]
             for which in (0, 1):
                 aside(c, j, which).start()
 
     def finish(c):
         rows = strip(x_me)
-        value = own_half[c, rows] + away_in[c, rows].astype(F32)
+        value = own_half[c % keep, rows] + away_in[c, rows].astype(F32)
         square = sq_half[c, rows] + sq_away_in[c, rows]
         for j in range(1, n_x):
             for which in (0, 1):
@@ -270,7 +273,7 @@
             jnp.dot(p, values[:, cut], preferred_element_type=F32) for p, cut in zip(probs, cuts)
         ]
         for value, weight, cut in zip(mixed, weights, cuts):
-            att[c, own, :, cut] = (value / weight * visible).astype(BF)
+            att[c * n_seq + own, :, cut] = (value / weight * visible).astype(BF)
         for j in range(1, n_x):
             to_x(c, j).start()
         to_core(c, x_me, 0).start()
@@ -281,20 +284,34 @@
         @pl.loop(0, width // tile)
         def _(t):
             cols = pl.ds(pl.multiple_of(t * tile, tile), tile)
-            rows = att[c].reshape(rows_all, qwidth)
-            value = jnp.dot(rows, wo[:qwidth, cols], preferred_element_type=F32).astype(BF)
-            for b in range(n_seq):
-                part[c * n_seq + b, :, cols] = value[b * sub : (b + 1) * sub]
+            rows = att[pl.ds(c * n_seq, n_seq)].reshape(rows_all, qwidth)
+            value = jnp.dot(rows, wo[:qwidth, cols], preferred_element_type=F32)
+            mixed_rows[:, cols] = value.astype(BF)
+
+        for j in range(n_x):
+            to_core(c, x_me, j).wait_send()
+        for j in range(1, n_x):
+            to_x(c, j).wait_send()
+        for b in range(n_seq):
+            part[c * n_seq + b] = mixed_rows[b * sub : (b + 1) * sub]
 
     def gather(p):
-        @pl.when(depth > 0)
-        def _():
-            inward(p).wait_recv()
-            part[p] = (part[p].astype(F32) + came[p].astype(F32)).astype(BF)
-
-        @pl.when(depth < half - 1)
-        def _():
-            inward(p).start()
+        for early in (True, False)[: 1 + (first < total)]:
+            @pl.when((p < first) == early)
+            def _(early=early):
+                @pl.when(depth > 0)
+                def _():
+                    inward(p, early).wait_recv()
+                    part[p] = (part[p].astype(F32) + landing(p, early)[...].astype(F32)).astype(BF)
+
+                @pl.when(depth < half - 1)
+                def _():
+                    if not early:
+                        @pl.when(p == first)
+                        def _():
+                            pl.semaphore_wait(free_sem, 1)
+
+                    inward(p, early).start()
 
         @pl.when(depth == half - 1)
         def _():
@@ -331,26 +348,31 @@
                 page_piece(j, other_z(k), k - 1).start()
 
     def share_page():
-        for j in range(owners):
+        for k in range(owners):
+            j = (me // stride + k) % owners
+
             @pl.when(me != j * stride)
             def _(j=j):
                 page_piece(j, j * stride, 0).wait_recv()
 
-        for j in range(1, n_x):
-            page_x(j).start()
-        page_core(x_me, 0).start()
+            for i in range(1, n_x):
+                page_x(i, j).start()
+            page_core(x_me, 0, j).start()
         page_ref[...] = pages[seq_me]
 
     def pass_pages():
-        for j in range(1, n_x):
-            page_from_x(j).wait_recv()
-            page_core(other_x(j), j).start()
+        for k in range(owners):
+            j = (me // stride + k) % owners
+            for i in range(1, n_x):
+                page_from_x(i, j).wait_recv()
+                page_core(other_x(i), i, j).start()
 
     def keys_values():
         load_k.wait()
         load_v.wait()
         for x in range(n_x):
-            page_from_core(x).wait_recv()
+            for k in range(owners):
+                page_from_core(x, k).wait_recv()
         rows = pages[...].reshape(n_seq * lat_rows, vis)
         tile = math.gcd(qwidth, 1024)
         for base, target in ((0, keys), (vis, values)):
@@ -365,7 +387,7 @@
 
     load_text(0).start()
     load_q.start()
-    for c in range(1, min(RING, count)):
+    for c in range(1, count):
         load_text(c).start()
     load_k.start()
     load_v.start()
@@ -401,6 +423,14 @@
         def _():
             project(s)
 
+            if first < total:
+                @pl.when(jnp.logical_and(s == count - 1, depth > 0))
+                def _():
+                    pl.semaphore_signal(
+                        free_sem, inc=1, device_id={"tensor": outer},
+                        device_id_type=pl.DeviceIdType.MESH,
+                    )
+
         later = jnp.maximum(s - LATER, 0)
 
         @pl.when(jnp.logical_or(s == EARLY, jnp.logical_and(later >= 1, later < count)))
@@ -447,28 +477,22 @@
 
     @pl.loop(0, total)
     def _(p):
-        inward(p).wait_send()
+        across(p).wait_send()
 
         @pl.when(depth > 0)
         def _():
             outward(p).wait_send()
-
-    @pl.loop(0, count)
-    def _(c):
-        for j in range(n_x):
-            to_core(c, x_me, j).wait_send()
-        for j in range(1, n_x):
-            to_x(c, j).wait_send()
 
     for c in range(max(count - RING, 0), count):
         for which in (0, 1):
             away(c, which).wait_send()
             for j in range(1, n_x):
                 aside(c, j, which).wait_send()
-    for j in range(n_x):
-        page_core(x_me, j).wait_send()
-    for j in range(1, n_x):
-        page_x(j).wait_send()
+    for k in range(owners):
+        for j in range(n_x):
+            page_core(x_me, j, k).wait_send()
+        for j in range(1, n_x):
+            page_x(j, k).wait_send()
     for j in range(owners):
         @pl.when(me != j * stride)
         def _(j=j):
@@ -490,16 +514,17 @@
     pieces = count * n_seq
     owners = math.gcd(n, lat_rows // 16)
     shared = qwidth == width and qwidth <= 2 * vis
+    first = min(pieces, n_seq) if shared and pieces * sub <= feat else pieces
     dma = pltpu.SemaphoreType.DMA
-    vmem, anywhere = pl.BlockSpec(memory_space=pltpu.VMEM), pl.BlockSpec(memory_space=pl.ANY)
+    vmem, anywhere = pl.BlockSpec(memory_space=pltpu.VMEM), pl.BlockSpec(memory_space=pltpu.HBM)
     others = max(n_x - 1, 1)
     half_rows = n_x * sub
+    stay = [pltpu.with_memory_space_constraint(v, pltpu.HBM) for v in (text, wq, wk, wv, wo)]
     scratch = [
         ((feat, qwidth), BF),
         ((2 * vis, qwidth), BF),
         ((16, 128) if shared else (qwidth, width), BF),
-        ((RING, n_seq * sub, feat), BF),
-        ((count, half_rows, qwidth), F32),
+        ((min(count, LEAD + 2), half_rows, qwidth), F32),
         ((RING, half_rows, qwidth), BF),
         ((count, half_rows, qwidth), BF),
         ((RING, others, sub, qwidth), BF),
@@ -514,22 +539,24 @@
         ((n_seq * lat_rows, qwidth), BF),
         ((n_seq, lat_rows, vis), BF),
         ((n, lat_rows // owners, vis), F32),
-        ((count, n_seq, sub, qwidth), BF),
-        ((pieces, sub, width), BF),
-        ((pieces, sub, width), BF),
+        ((pieces, sub, qwidth), BF),
+        ((1, 16, 128) if shared else (pieces, sub, width), BF),
+        ((first, sub, width), BF),
+        ((n_seq * sub, width), BF),
     ]
     return pl.pallas_call(
-        functools.partial(flow_kernel, (n_x, n, count, sub, owners, shared)),
+        functools.partial(flow_kernel, (n_x, n, count, sub, owners, shared, first)),
         out_shape=(
             jax.ShapeDtypeStruct((tokens, width), BF),
+            jax.ShapeDtypeStruct((tokens, feat), BF),
             jax.ShapeDtypeStruct((lat_rows, vis), BF),
         ),
         in_specs=[vmem] * 5 + [anywhere] * 5,
-        out_specs=(vmem, vmem),
+        out_specs=(vmem, vmem, vmem),
         scratch_shapes=[pltpu.VMEM(shape, kind) for shape, kind in scratch]
         + [
             dma((4,)),
-            dma((RING,)),
+            dma((count,)),
             dma((2, RING)),
             dma((2, count)),
             dma((2, RING, others)),
@@ -538,39 +565,57 @@
             dma((n,)),
             dma((n,)),
             dma((owners,)),
-            dma((2 * n_x,)),
-            dma((n_x,)),
-            dma((n_x,)),
+            dma((2 * n_x, owners)),
+            dma((n_x, owners)),
+            dma((n_x, owners)),
             dma((count, n_x)),
             dma((count, n_x)),
             dma((count, 2 * n_x - 1)),
         ]
-        + [dma((pieces,))] * 4,
+        + [dma((pieces,))] * 4
+        + [pltpu.SemaphoreType.REGULAR],
         compiler_params=pltpu.CompilerParams(
-            collective_id=0, has_side_effects=True, vmem_limit_bytes=63 << 20
+            collective_id=0, has_side_effects=True, vmem_limit_bytes=41984 << 10
         ),
         name="flow",
-    )(partial_value, latents, gain, img, owner, text, wq, wk, wv, wo)
-
-
-def close_kernel(rows, text_ref, gate_ref, branch_ref, out_ref):
-    at = pl.multiple_of(pl.program_id(0) * rows, rows)
-    branch = branch_ref[pl.ds(at, rows)].astype(F32)
-    out_ref[...] = text_ref[...].astype(F32) + jnp.tanh(gate_ref[...]) * branch
+    )(partial_value, latents, gain, img, owner, *stay)
+
+
+def close_kernel(rows, slots, text_ref, gate_ref, branch_ref, out_ref, buf, sem):
+    steps = text_ref.shape[0] // rows
+    gate = jnp.tanh(gate_ref[...])
+
+    def put(i):
+        return pltpu.make_async_copy(
+            buf.at[i % slots], out_ref.at[pl.ds(i * rows, rows)], sem.at[i % slots]
+        )
+
+    @pl.loop(0, steps)
+    def _(i):
+        @pl.when(i >= slots)
+        def _():
+            put(i - slots).wait()
+
+        at = pl.ds(pl.multiple_of(i * rows, rows), rows)
+        buf[i % slots] = text_ref[at].astype(F32) + gate * branch_ref[at].astype(F32)
+        put(i).start()
+
+    @pl.loop(max(steps - slots, 0), steps)
+    def _(i):
+        put(i).wait()
 
 
 def close(text, gate, branch):
     tokens, width = text.shape
-    rows = math.gcd(tokens, 128)
-    block = pl.BlockSpec((rows, width), lambda i: (i, 0))
+    rows = math.gcd(tokens, 64)
     whole = pl.BlockSpec(memory_space=pltpu.VMEM)
     return pl.pallas_call(
-        functools.partial(close_kernel, rows),
+        functools.partial(close_kernel, rows, 4),
         out_shape=jax.ShapeDtypeStruct((tokens, width), F32),
-        grid=(tokens // rows,),
-        in_specs=[block, whole, whole],
-        out_specs=block,
-        compiler_params=pltpu.CompilerParams(vmem_limit_bytes=16 << 20),
+        in_specs=[whole] * 3,
+        out_specs=pl.BlockSpec(memory_space=pl.ANY),
+        scratch_shapes=[pltpu.VMEM((4, rows, width), F32), pltpu.SemaphoreType.DMA((4,))],
+        compiler_params=pltpu.CompilerParams(vmem_limit_bytes=4 << 20),
         name="close",
     )(text, gate, branch)
 
@@ -604,7 +649,7 @@
         ).reshape(-1, 1)
         partial_value = resample(patches, latents, wq_res, wk_res, wv_res, wo_res)
         owner = jnp.arange(n_seq * partial_value.shape[0], dtype=jnp.int32) // lat_count
-        branch, page_latents = flow(
+        branch, text, page_latents = flow(
             partial_value, latents, norm_gain[None, :], img, owner[None, :], text,
             wq_x, wk_x, wv_x, wo_x, n_x, n_tensor,
         )

time: 220 us -> 211 us (0.959)
  local copies, waits for them, and re-layouts: 10.8 us -> 3.43 us
    unnamed x13 -> x9, local copies, waits for them, and re-layouts: 6.94 us -> 0.7 us
where the time goes in v1:
time: 211 us; the launch traced here: 210 us
  Pallas kernels  200 us (95%)
  matrix products  5.96 us (3%)
  local copies, waits for them, and re-layouts  3.43 us (2%)
    pallas_call x1, Pallas kernels, flow(): pl.pallas_call(functools.partial(flow_kernel, (n_x, n, count, sub, owners...  194 us
    pallas_call x1, Pallas kernels, close(): pl.pallas_call(functools.partial(close_kernel, rows, 4), out_shape=jax.Sh...  5.75 us

profile of v1, /device:TPU:0, one launch (start us, length us, event | category | flops | bytes accessed | tf_op | source)
XLA Modules:
  0.0 210.3 jit_solution(11637075961519951173)
XLA Ops:
  0.6 0.0 copy-start
  0.6 0.0 copy-start.1
  0.7 0.0 copy-start.3
  0.7 0.8 broadcast_in_dim.4.refs_2_
  1.5 0.8 reshape.83
  2.3 1.6 convolution_convert_fusion.2
  3.9 0.1 reshape.80
  4.0 0.2 reshape.85.refs_3_
  4.2 0.0 copy-done
  4.2 1.6 convolution_convert_fusion.1
  5.9 0.3 reshape.79
  6.2 0.3 fusion.7
  6.5 0.2 convert_reduce_fusion
  6.7 1.9 convolution_convert_fusion
  8.7 0.3 reshape.82
  9.0 0.3 fusion.2
  9.3 0.1 copy.22
  9.3 0.1 convert_element_type.35
  9.4 0.0 copy-done.3
  9.5 0.3 fusion.8.refs_0_
  9.7 0.0 copy-done.1
  9.7 0.0 copy-start.2
  9.8 194.1 %flow.1 = (bf16[1536,2048]{1,0:T(8,128)(2,1)S(1)}, bf16[1536,2048]{1,0:T(8,128)(2,1)S(1)}, bf16[64,1280]{1,0:T(8,128)(2,1)S(1)}) custom-call(f32[64,1280]{1,0:T(8,128)S(1)} %fusion.8.refs_0_, bf16[64,1280]{1,0:T(8,128)(2,1)S(1)} %copy-done.1, bf16[1,2048]{1,0:T(2,128)(2,1)S(1)} %broadcast_in_dim.4.refs_2_, s32[384,1]{1,0:T(8,128)S(1)} %reshape.85.refs_3_, ...), custom_call_target="tpu_custom_call" | custom-call | tf_op jit(solution)/shard_map/flow/pallas_call | solution.py:547
  203.8 0.0 copy-done.2
  203.8 5.7 %close.1 = f32[1536,2048]{1,0:T(8,128)} custom-call(bf16[1536,2048]{1,0:T(8,128)(2,1)S(1)} %get-tuple-element.5.text_ref, f32[1,2048]{1,0:T(1,128)S(1)} %bitcast.20, bf16[1536,2048]{1,0:T(8,128)(2,1)S(1)} %get-tuple-element.6.branch_ref), custom_call_target="tpu_custom_call" | custom-call | tf_op jit(solution)/shard_map/close/pallas_call | solution.py:612
  209.6 0.7 copy.35
  (2 shorter events, 0.0 us)
Async XLA Ops:
  0.6 3.6 %copy-start = (bf16[1280,384]{1,0:T(8,128)(2,1)S(1)}, bf16[1280,384]{1,0:T(8,128)(2,1)}, u32[]{:S(2)}) copy-start(bf16[1280,384]{1,0:T(8,128)(2,1)} %param.17) | copy-start | bytes 2949124
  0.6 9.1 %copy-start.1 = (bf16[64,1280]{1,0:T(8,128)(2,1)S(1)}, bf16[64,1280]{1,0:T(8,128)(2,1)}, u32[]{:S(2)}) copy-start(bf16[64,1280]{1,0:T(8,128)(2,1)} %refs_1_.1) | copy-start | bytes 491524
  0.7 8.8 %copy-start.3 = (bf16[384,1280]{1,0:T(8,128)(2,1)S(1)}, bf16[384,1280]{1,0:T(8,128)(2,1)}, u32[]{:S(2)}) copy-start(bf16[384,1280]{1,0:T(8,128)(2,1)} %param.19) | copy-start | bytes 2949124
  9.7 194.1 %copy-start.2 = (f32[2048]{0:T(1024)S(1)}, f32[2048]{0:T(1024)}, u32[]{:S(2)}) copy-start(f32[2048]{0:T(1024)} %param.26) | copy-start | bytes 24580

commit v2 on v1

--- a/solution.py
+++ b/solution.py
@@ -12,9 +12,13 @@
 RES_HEAD = 96
 PATCH_IMG = 257
 SUB = 32
-LEAD = 9
-SUM_STEP, PAGE_STEP, PASS_STEP = 3, 6, 8
-EARLY, LATER = 3, 7
+CUT = 2
+TILES = 2
+SOON = 2
+LAG = 3
+LEAD = 12
+SUM_STEP, PAGE_STEP, PASS_STEP = 4, 8, 11
+EARLY, AHEAD, LATER = 2, 2, 11
 RING = 2
 BF = jnp.bfloat16
 F32 = jnp.float32
@@ -55,7 +59,7 @@
 
 
 def flow_kernel(dims, *refs):
-    n_x, n, count, sub, owners, shared, first = dims
+    n_x, n, count, sub, owners, shared, tight = dims
     (part_ref, lat_ref, gain_ref, img_ref, own_ref, text_ref, wq_ref, wk_ref, wv_ref, wo_ref) = refs[:10]
     out_ref, text, page_ref = refs[10:13]
     (wq, wkv, late, own_half, away_out, away_in, x_out, x_in, sq_half, sq_away_out, sq_away_in,
@@ -64,7 +68,9 @@
      pg_send, pg_x, pg_core, side_sem, core_sem, block_sem, in_sem, back_sem, inward_sem,
      outward_sem, free_sem) = refs[35:]
     n_seq, half = 2 * n_x, n // 2
-    total = count * n_seq
+    cut = CUT if sub % (16 * CUT) == 0 else 1
+    size, per = sub // cut, n_seq * cut
+    total = count * per
     keep = own_half.shape[0]
     rows_all, rows_half = n_seq * sub, n_x * sub
     seq_me, me = lax.axis_index("seq"), lax.axis_index("tensor")
@@ -74,7 +80,7 @@
     side = me // half
     depth = me * (1 - side) + (n - 1 - me) * side
     inner, outer = me + 1 - 2 * side, me - 1 + 2 * side
-    lag = 2 + 4 * (half - 1 - depth)
+    lag = LAG + 5 * (half - 1 - depth)
     feat, qwidth = wq.shape
     width = wo_ref.shape[1]
     heads = qwidth // HEAD
@@ -172,19 +178,20 @@
         return remote(ref, ref, block_sem.at[c, n_x + j - 1], side_sem.at[c, x], seq=2 * x + core)
 
     def rows_of(p):
-        return pl.ds(pl.multiple_of(p * sub, sub), sub)
-
-    def landing(p, early):
-        if early:
-            return came.at[p]
-        return wq.at[pl.ds(pl.multiple_of((p - first) * sub, sub), sub)]
-
-    def inward(p, early):
-        return remote(part.at[p], landing(p, early), inward_sem.at[p], in_sem.at[p], tensor=inner)
+        return pl.ds(pl.multiple_of(p * size, size), size)
+
+    def piece(p):
+        return part.at[p // cut, pl.ds(pl.multiple_of((p % cut) * size, size), size)]
+
+    def landing(p):
+        return (wq if tight else came).at[rows_of(p)]
+
+    def inward(p):
+        return remote(piece(p), landing(p), inward_sem.at[p], in_sem.at[p], tensor=inner)
 
     def across(p):
         return remote(
-            part.at[p], out_ref.at[rows_of(p)], inward_sem.at[p], back_sem.at[p], tensor=inner
+            piece(p), out_ref.at[rows_of(p)], inward_sem.at[p], back_sem.at[p], tensor=inner
         )
 
     def outward(p):
@@ -278,16 +285,14 @@
             to_x(c, j).start()
         to_core(c, x_me, 0).start()
 
-    def product(c):
-        tile = math.gcd(width, 1024)
-
-        @pl.loop(0, width // tile)
-        def _(t):
-            cols = pl.ds(pl.multiple_of(t * tile, tile), tile)
-            rows = att[pl.ds(c * n_seq, n_seq)].reshape(rows_all, qwidth)
-            value = jnp.dot(rows, wo[:qwidth, cols], preferred_element_type=F32)
-            mixed_rows[:, cols] = value.astype(BF)
-
+    def product(c, t):
+        tile = width // TILES
+        cols = slice(t * tile, (t + 1) * tile)
+        rows = att[pl.ds(c * n_seq, n_seq)].reshape(rows_all, qwidth)
+        value = jnp.dot(rows, wo[:qwidth, cols], preferred_element_type=F32)
+        mixed_rows[:, cols] = value.astype(BF)
+
+    def replace(c):
         for j in range(n_x):
             to_core(c, x_me, j).wait_send()
         for j in range(1, n_x):
@@ -296,22 +301,19 @@
             part[c * n_seq + b] = mixed_rows[b * sub : (b + 1) * sub]
 
     def gather(p):
-        for early in (True, False)[: 1 + (first < total)]:
-            @pl.when((p < first) == early)
-            def _(early=early):
-                @pl.when(depth > 0)
+        @pl.when(depth > 0)
+        def _():
+            inward(p).wait_recv()
+            piece(p)[...] = (piece(p)[...].astype(F32) + landing(p)[...].astype(F32)).astype(BF)
+
+        @pl.when(depth < half - 1)
+        def _():
+            if tight:
+                @pl.when(p == 0)
                 def _():
-                    inward(p, early).wait_recv()
-                    part[p] = (part[p].astype(F32) + landing(p, early)[...].astype(F32)).astype(BF)
-
-                @pl.when(depth < half - 1)
-                def _():
-                    if not early:
-                        @pl.when(p == first)
-                        def _():
-                            pl.semaphore_wait(free_sem, 1)
-
-                    inward(p, early).start()
+                    pl.semaphore_wait(free_sem, 1)
+
+            inward(p).start()
 
         @pl.when(depth == half - 1)
         def _():
@@ -323,7 +325,7 @@
         @pl.when(depth == half - 1)
         def _():
             rows = rows_of(p)
-            out_ref[rows] = (part[p].astype(F32) + out_ref[rows].astype(F32)).astype(BF)
+            out_ref[rows] = (piece(p)[...].astype(F32) + out_ref[rows].astype(F32)).astype(BF)
 
         @pl.when(depth > 0)
         def _():
@@ -387,13 +389,8 @@
 
     load_text(0).start()
     load_q.start()
-    for c in range(1, count):
+    for c in range(1, min(SOON, count)):
         load_text(c).start()
-    load_k.start()
-    load_v.start()
-    if not shared:
-        load_o.start()
-
     barrier = pltpu.get_barrier_semaphore()
 
     def greet(**where):
@@ -412,8 +409,14 @@
             lat_piece(j).start()
 
     load_q.wait()
-
-    @pl.loop(0, count + LEAD + 1)
+    for c in range(SOON, count):
+        load_text(c).start()
+    load_k.start()
+    load_v.start()
+    if not shared:
+        load_o.start()
+
+    @pl.loop(0, count + LEAD + 2)
     def _(s):
         pl.when(s == SUM_STEP)(sum_latents)
         pl.when(s == PAGE_STEP)(share_page)
@@ -423,7 +426,7 @@
         def _():
             project(s)
 
-            if first < total:
+            if tight:
                 @pl.when(jnp.logical_and(s == count - 1, depth > 0))
                 def _():
                     pl.semaphore_signal(
@@ -431,15 +434,28 @@
                         device_id_type=pl.DeviceIdType.MESH,
                     )
 
-        later = jnp.maximum(s - LATER, 0)
-
-        @pl.when(jnp.logical_or(s == EARLY, jnp.logical_and(later >= 1, later < count)))
-        def _():
-            scatter(later)
+        @pl.when(jnp.logical_and(s >= EARLY, s < EARLY + min(AHEAD, count)))
+        def _():
+            scatter(s - EARLY)
 
         c = s - LEAD - 1
-
-        @pl.when(c >= 0)
+        ready = jnp.logical_and(c >= 0, c < count)
+
+        def pieces(low, high):
+            @pl.when(c >= 1)
+            def _():
+                @pl.loop(low, high)
+                def _(b):
+                    p = (c - 1) * per + b
+                    gather(p)
+
+                    @pl.when(jnp.logical_and(depth > 0, p >= lag))
+                    def _():
+                        spread(p - lag)
+
+        pieces(0, per // 2)
+
+        @pl.when(ready)
         def _():
             for j in range(1, n_x):
                 from_x(c, j).wait_recv()
@@ -452,22 +468,26 @@
             finish(s - LEAD)
             attend(s - LEAD)
 
+        @pl.when(jnp.logical_and(s >= LATER + AHEAD, s < LATER + count))
+        def _():
+            scatter(s - LATER)
+
         pl.when(c == 0)(load_o.wait)
-
-        @pl.when(c >= 0)
+        pieces(per // 2, 3 * per // 4)
+
+        @pl.when(ready)
         def _():
             for x in range(n_x):
                 from_core(c, x).wait_recv()
-            product(c)
-
-            @pl.loop(0, n_seq)
-            def _(b):
-                p = c * n_seq + b
-                gather(p)
-
-                @pl.when(jnp.logical_and(depth > 0, p >= lag))
-                def _():
-                    spread(p - lag)
+            product(c, 0)
+
+        pieces(3 * per // 4, per)
+
+        @pl.when(ready)
+        def _():
+            for t in range(1, TILES):
+                product(c, t)
+            replace(c)
 
     @pl.loop(0, total)
     def _(p):
@@ -511,10 +531,11 @@
     lat_rows, vis = partial_value.shape
     sub = math.gcd(tokens // n_seq, SUB)
     count = tokens // (n_seq * sub)
-    pieces = count * n_seq
+    blocks = count * n_seq
+    pieces = blocks * (CUT if sub % (16 * CUT) == 0 else 1)
     owners = math.gcd(n, lat_rows // 16)
     shared = qwidth == width and qwidth <= 2 * vis
-    first = min(pieces, n_seq) if shared and pieces * sub <= feat else pieces
+    tight = qwidth == width and tokens <= feat
     dma = pltpu.SemaphoreType.DMA
     vmem, anywhere = pl.BlockSpec(memory_space=pltpu.VMEM), pl.BlockSpec(memory_space=pltpu.HBM)
     others = max(n_x - 1, 1)
@@ -539,13 +560,13 @@
         ((n_seq * lat_rows, qwidth), BF),
         ((n_seq, lat_rows, vis), BF),
         ((n, lat_rows // owners, vis), F32),
-        ((pieces, sub, qwidth), BF),
-        ((1, 16, 128) if shared else (pieces, sub, width), BF),
-        ((first, sub, width), BF),
+        ((blocks, sub, qwidth), BF),
+        ((1, 16, 128) if shared else (blocks, sub, width), BF),
+        ((16, 128) if tight else (tokens, width), BF),
         ((n_seq * sub, width), BF),
     ]
     return pl.pallas_call(
-        functools.partial(flow_kernel, (n_x, n, count, sub, owners, shared, first)),
+        functools.partial(flow_kernel, (n_x, n, count, sub, owners, shared, tight)),
         out_shape=(
             jax.ShapeDtypeStruct((tokens, width), BF),
             jax.ShapeDtypeStruct((tokens, feat), BF),
@@ -581,15 +602,18 @@
     )(partial_value, latents, gain, img, owner, *stay)
 
 
-def close_kernel(rows, slots, text_ref, gate_ref, branch_ref, out_ref, buf, sem):
+def close_kernel(rows, slots, text_ref, gate_ref, branch_ref, page_ref, out_ref, page_out, buf, sem, page_sem):
     steps = text_ref.shape[0] // rows
     gate = jnp.tanh(gate_ref[...])
+    page = pltpu.make_async_copy(page_ref, page_out, page_sem)
 
     def put(i):
         return pltpu.make_async_copy(
             buf.at[i % slots], out_ref.at[pl.ds(i * rows, rows)], sem.at[i % slots]
         )
 
+    page.start()
+
     @pl.loop(0, steps)
     def _(i):
         @pl.when(i >= slots)
@@ -604,20 +628,30 @@
     def _(i):
         put(i).wait()
 
-
-def close(text, gate, branch):
+    page.wait()
+
+
+def close(text, gate, branch, page):
     tokens, width = text.shape
     rows = math.gcd(tokens, 64)
-    whole = pl.BlockSpec(memory_space=pltpu.VMEM)
+    slots = 8
+    whole, anywhere = pl.BlockSpec(memory_space=pltpu.VMEM), pl.BlockSpec(memory_space=pl.ANY)
     return pl.pallas_call(
-        functools.partial(close_kernel, rows, 4),
-        out_shape=jax.ShapeDtypeStruct((tokens, width), F32),
-        in_specs=[whole] * 3,
-        out_specs=pl.BlockSpec(memory_space=pl.ANY),
-        scratch_shapes=[pltpu.VMEM((4, rows, width), F32), pltpu.SemaphoreType.DMA((4,))],
-        compiler_params=pltpu.CompilerParams(vmem_limit_bytes=4 << 20),
+        functools.partial(close_kernel, rows, slots),
+        out_shape=(
+            jax.ShapeDtypeStruct((tokens, width), F32),
+            jax.ShapeDtypeStruct(page.shape, page.dtype),
+        ),
+        in_specs=[whole] * 4,
+        out_specs=(anywhere, anywhere),
+        scratch_shapes=[
+            pltpu.VMEM((slots, rows, width), F32),
+            pltpu.SemaphoreType.DMA((slots,)),
+            pltpu.SemaphoreType.DMA,
+        ],
+        compiler_params=pltpu.CompilerParams(vmem_limit_bytes=8 << 20),
         name="close",
-    )(text, gate, branch)
+    )(text, gate, branch, page)
 
 
 def make_shards(n_seq, n_tensor):
@@ -653,7 +687,7 @@
             partial_value, latents, norm_gain[None, :], img, owner[None, :], text,
             wq_x, wk_x, wv_x, wo_x, n_x, n_tensor,
         )
-        return close(text, gate_x[None, :], branch), page_latents
+        return close(text, gate_x[None, :], branch, page_latents)
 
     return shards
 

time: 211 us -> 203 us (0.962)
  Pallas kernels: 200 us -> 193 us
    pallas_call x1, Pallas kernels: 194 us -> 188 us  [flow(): pl.pallas_call(functools.partial(flow_kernel, (n_x, n, count, sub, owners...]
where the time goes in v2:
time: 203 us; the launch traced here: 202 us
  Pallas kernels  193 us (95%)
  matrix products  5.96 us (3%)
  local copies, waits for them, and re-layouts  2.76 us (1%)
    pallas_call x1, Pallas kernels, flow(): pl.pallas_call(functools.partial(flow_kernel, (n_x, n, count, sub, owners...  188 us
    pallas_call x1, Pallas kernels, close(): pl.pallas_call(functools.partial(close_kernel, rows, slots), out_shape=(j...  4.7 us

profile of v2, /device:TPU:0, one launch (start us, length us, event | category | flops | bytes accessed | tf_op | source)
XLA Modules:
  0.0 202.4 jit_solution(1299596187262882207)
XLA Ops:
  0.6 0.0 copy-start
  0.6 0.0 copy-start.1
  0.7 0.0 copy-start.3
  0.7 0.8 broadcast_in_dim.4.refs_2_
  1.5 0.8 reshape.83
  2.3 1.6 convolution_convert_fusion.2
  3.9 0.1 reshape.80
  4.0 0.2 reshape.85.refs_3_
  4.2 0.0 copy-done
  4.2 1.6 convolution_convert_fusion.1
  5.9 0.3 reshape.79
  6.2 0.3 fusion.7
  6.5 0.2 convert_reduce_fusion
  6.7 1.9 convolution_convert_fusion
  8.7 0.3 reshape.82
  9.0 0.3 fusion.2
  9.3 0.1 copy.22
  9.3 0.1 convert_element_type.35
  9.4 0.0 copy-done.3
  9.5 0.3 fusion.8.refs_0_
  9.7 0.0 copy-done.1
  9.7 0.0 copy-start.2
  9.8 187.9 %flow.1 = (bf16[1536,2048]{1,0:T(8,128)(2,1)S(1)}, bf16[1536,2048]{1,0:T(8,128)(2,1)S(1)}, bf16[64,1280]{1,0:T(8,128)(2,1)S(1)}) custom-call(f32[64,1280]{1,0:T(8,128)S(1)} %fusion.8.refs_0_, bf16[64,1280]{1,0:T(8,128)(2,1)S(1)} %copy-done.1, bf16[1,2048]{1,0:T(2,128)(2,1)S(1)} %broadcast_in_dim.4.refs_2_, s32[384,1]{1,0:T(8,128)S(1)} %reshape.85.refs_3_, ...), custom_call_target="tpu_custom_call" | custom-call | tf_op jit(solution)/shard_map/flow/pallas_call | solution.py:568
  197.7 0.0 copy-done.2
  197.7 4.7 %close.1 = (f32[1536,2048]{1,0:T(8,128)}, bf16[64,1280]{1,0:T(8,128)(2,1)}) custom-call(bf16[1536,2048]{1,0:T(8,128)(2,1)S(1)} %get-tuple-element.5.text_ref, f32[1,2048]{1,0:T(1,128)S(1)} %bitcast.20, bf16[1536,2048]{1,0:T(8,128)(2,1)S(1)} %get-tuple-element.6.branch_ref, bf16[64,1280]{1,0:T(8,128)(2,1)S(1)} %get-tuple-element.7.page_ref), custom_call_target="tpu_custom_call" | custom-call | tf_op jit(solution)/shard_map/close/pallas_call | solution.py:639
  (2 shorter events, 0.0 us)
Async XLA Ops:
  0.6 3.6 %copy-start = (bf16[1280,384]{1,0:T(8,128)(2,1)S(1)}, bf16[1280,384]{1,0:T(8,128)(2,1)}, u32[]{:S(2)}) copy-start(bf16[1280,384]{1,0:T(8,128)(2,1)} %param.17) | copy-start | bytes 2949124
  0.6 9.1 %copy-start.1 = (bf16[64,1280]{1,0:T(8,128)(2,1)S(1)}, bf16[64,1280]{1,0:T(8,128)(2,1)}, u32[]{:S(2)}) copy-start(bf16[64,1280]{1,0:T(8,128)(2,1)} %refs_1_.1) | copy-start | bytes 491524
  0.7 8.8 %copy-start.3 = (bf16[384,1280]{1,0:T(8,128)(2,1)S(1)}, bf16[384,1280]{1,0:T(8,128)(2,1)}, u32[]{:S(2)}) copy-start(bf16[384,1280]{1,0:T(8,128)(2,1)} %param.19) | copy-start | bytes 2949124
  9.7 187.9 %copy-start.2 = (f32[2048]{0:T(1024)S(1)}, f32[2048]{0:T(1024)}, u32[]{:S(2)}) copy-start(f32[2048]{0:T(1024)} %param.26) | copy-start | bytes 24580

commit v3 on v2

--- a/solution.py
+++ b/solution.py
@@ -17,56 +17,23 @@
 SOON = 2
 LAG = 3
 LEAD = 12
-SUM_STEP, PAGE_STEP, PASS_STEP = 4, 8, 11
+SUM_STEP, PAGE_STEP, PASS_STEP = 4, 7, 10
 EARLY, AHEAD, LATER = 2, 2, 11
 RING = 2
 BF = jnp.bfloat16
 F32 = jnp.float32
 
 
-def resample(patches, latents, wq_res, wk_res, wv_res, wo_res):
-    inv_res = 1.0 / math.sqrt(RES_HEAD)
-    lat_count = latents.shape[0]
-    img_count = patches.shape[0] // PATCH_IMG
-    heads_res = wq_res.shape[1] // RES_HEAD
-    queries = (
-        jnp.dot(latents, wq_res, preferred_element_type=F32)
-        .astype(BF)
-        .reshape(lat_count, heads_res, RES_HEAD)
-    )
-    page_keys = (
-        jnp.dot(patches, wk_res, preferred_element_type=F32)
-        .astype(BF)
-        .reshape(img_count, PATCH_IMG, heads_res, RES_HEAD)
-    )
-    page_values = (
-        jnp.dot(patches, wv_res, preferred_element_type=F32)
-        .astype(BF)
-        .reshape(img_count, PATCH_IMG, heads_res, RES_HEAD)
-    )
-    scores = jnp.einsum("lhd,iphd->ihlp", queries, page_keys, preferred_element_type=F32) * inv_res
-    summit = jnp.max(scores, axis=3, keepdims=True)
-    weights = jnp.exp(scores - summit).astype(BF)
-    totals = jnp.sum(weights, axis=3, dtype=F32)
-    blended = jnp.einsum("ihlp,iphd->ihld", weights, page_values, preferred_element_type=F32)
-    pooled = (
-        (blended / totals[:, :, :, None])
-        .transpose(0, 2, 1, 3)
-        .reshape(img_count * lat_count, heads_res * RES_HEAD)
-        .astype(BF)
-    )
-    return jnp.dot(pooled, wo_res, preferred_element_type=F32)
-
-
 def flow_kernel(dims, *refs):
-    n_x, n, count, sub, owners, shared, tight = dims
-    (part_ref, lat_ref, gain_ref, img_ref, own_ref, text_ref, wq_ref, wk_ref, wv_ref, wo_ref) = refs[:10]
-    out_ref, text, page_ref = refs[10:13]
-    (wq, wkv, late, own_half, away_out, away_in, x_out, x_in, sq_half, sq_away_out, sq_away_in,
-     sq_x_out, sq_x_in, query, keys, values, pages, lat_in, att, second, came, mixed_rows) = refs[13:35]
-    (load_sem, text_sem, qc_send, qc_recv, qx_send, qx_recv, lat_send, lat_recv, pz_send, pz_recv,
+    n_x, n, count, sub, owners, shared, tight, roomy, windowed = dims
+    (patch_hbm, lat_hbm, gain_hbm, img_hbm, wqr_hbm, wkr_hbm, wvr_hbm, wor_hbm,
+     text_ref, wq_ref, wk_ref, wv_ref, wo_ref) = refs[:13]
+    out_ref, text, page_ref = refs[13:16]
+    (part_sum, part_ref, lat_ref, lat_own, gain_ref, img_ref, patch_ref, wqr, wkr, wvr, wor, wq, wkv, late, own_half, away_in, x_out, x_in, sq_half, sq_away_out, sq_away_in,
+     sq_x_out, sq_x_in, query, keys, values, pages, lat_in, att, second, came, mixed_rows) = refs[16:48]
+    (load_sem, res_sem, text_sem, qc_send, qc_recv, qx_send, qx_recv, lat_send, lat_recv, pz_send, pz_recv,
      pg_send, pg_x, pg_core, side_sem, core_sem, block_sem, in_sem, back_sem, inward_sem,
-     outward_sem, free_sem) = refs[35:]
+     outward_sem, free_sem) = refs[48:]
     n_seq, half = 2 * n_x, n // 2
     cut = CUT if sub % (16 * CUT) == 0 else 1
     size, per = sub // cut, n_seq * cut
@@ -90,6 +57,11 @@
     part_rows = lat_rows // owners
     stride = n // owners
     wo = wkv if shared else late
+    if roomy:
+        at = count * rows_all
+        mixed_rows = wq.at[pl.ds(at, rows_all)]
+        keys = wq.at[pl.ds(at + rows_all, n_seq * lat_rows)]
+        query = wq.at[pl.ds(at + rows_all + n_seq * lat_rows, sub)]
     part = att if shared else second
 
     def remote(src, dst, sent, got, **where):
@@ -113,6 +85,77 @@
     load_v = pltpu.make_async_copy(wv_ref, wkv.at[pl.ds(vis, vis)], load_sem.at[2])
     load_o = pltpu.make_async_copy(wo_ref, wo.at[pl.ds(0, qwidth)], load_sem.at[3])
 
+    res = wqr_hbm.shape[1]
+    lat_count = lat_hbm.shape[0]
+    if windowed:
+        wqr, wkr, wvr = (wkv.at[pl.ds(0, vis), pl.ds(k * res, res)] for k in range(3))
+        wor = wkv.at[pl.ds(vis, res), pl.ds(0, vis)]
+        lat_ref = wkv.at[pl.ds(vis + res, lat_count), pl.ds(0, vis)]
+    lat_from = (me // stride * part_rows) % lat_count
+    load_own = pltpu.make_async_copy(
+        lat_hbm.at[pl.ds(pl.multiple_of(lat_from, part_rows), part_rows)], lat_own, res_sem.at[8]
+    )
+    load_res = [
+        pltpu.make_async_copy(src, dst, res_sem.at[k])
+        for k, (src, dst) in enumerate((
+            (lat_hbm, lat_ref), (wqr_hbm, wqr), (patch_hbm, patch_ref), (wkr_hbm, wkr),
+            (wvr_hbm, wvr), (wor_hbm, wor), (gain_hbm, gain_ref), (img_hbm, img_ref),
+        ))
+    ]
+
+    def resample():
+        images = patch_ref.shape[0] // PATCH_IMG
+        whole = PATCH_IMG // 128 * 128
+        count_res = res // RES_HEAD
+        inv_res = 1.0 / math.sqrt(RES_HEAD)
+        load_res[0].wait()
+        load_res[1].wait()
+        lat_q = jnp.dot(lat_ref[...], wqr[...], preferred_element_type=F32).astype(BF).astype(F32)
+        column = lax.broadcasted_iota(jnp.int32, (1, res), 1)
+        inside = [
+            jnp.logical_and(column >= h * RES_HEAD, column < (h + 1) * RES_HEAD)
+            for h in range(count_res)
+        ]
+        stacked = jnp.concatenate([jnp.where(m, lat_q, 0.0) for m in inside], axis=0)
+        packed = stacked.astype(BF)
+        for k in range(2, 6):
+            load_res[k].wait()
+        for i in range(images):
+            base = i * PATCH_IMG
+            spans = [(base, whole)] + [(base + r, 1) for r in range(whole, PATCH_IMG)]
+
+            def both(w):
+                return [
+                    jnp.dot(patch_ref[at : at + rows], w[...], preferred_element_type=F32).astype(BF)
+                    for at, rows in spans
+                ]
+
+            page_k, page_v = both(wkr), both(wvr)
+            scores = lax.dot_general(
+                packed, page_k[0], (((1,), (1,)), ((), ())), preferred_element_type=F32
+            ) * inv_res
+            extra = [
+                jnp.sum(stacked * row.astype(F32), axis=1, keepdims=True) * inv_res
+                for row in page_k[1:]
+            ]
+            summit = jnp.max(scores, axis=1, keepdims=True)
+            for more in extra:
+                summit = jnp.maximum(summit, more)
+            weights = jnp.exp(scores - summit).astype(BF)
+            sums = jnp.sum(weights.astype(F32), axis=1, keepdims=True)
+            blended = jnp.dot(weights, page_v[0], preferred_element_type=F32)
+            for more, row in zip(extra, page_v[1:]):
+                weight = jnp.exp(more - summit).astype(BF).astype(F32)
+                sums = sums + weight
+                blended = blended + weight * row.astype(F32)
+            blended = blended / sums
+            pooled = jnp.zeros((lat_count, res), F32)
+            for h, m in enumerate(inside):
+                pooled = jnp.where(m, blended[h * lat_count : (h + 1) * lat_count], pooled)
+            value = jnp.dot(pooled.astype(BF), wor[...], preferred_element_type=F32)
+            part_sum[i * lat_count : (i + 1) * lat_count] = value
+            part_ref[i * lat_count : (i + 1) * lat_count] = value.astype(BF)
+
     def lat_piece(j):
         rows = pl.ds(j * part_rows, part_rows)
         return remote(
@@ -145,10 +188,16 @@
         ref = pages.at[2 * x + core, page_rows(k)]
         return remote(ref, ref, pg_send.at[n_x + j - 1, k], pg_x.at[x, k], seq=2 * x + core)
 
+    def outgoing(c):
+        return (count - 1) * n_seq + (c % RING) * n_x
+
     def away(c, which):
-        src, dst = (away_out, away_in) if which == 0 else (sq_away_out, sq_away_in)
+        if which == 0:
+            src, dst = att.at[pl.ds(outgoing(c), n_x)], away_in
+        else:
+            src, dst = sq_away_out.at[c % RING], sq_away_in
         return remote(
-            src.at[c % RING], dst.at[c], qc_send.at[which, c % RING], qc_recv.at[which, c], seq=partner
+            src, dst.at[c], qc_send.at[which, c % RING], qc_recv.at[which, c], seq=partner
         )
 
     def aside(c, j, which):
@@ -217,16 +266,21 @@
             [text[half_rows(2 * c + 1 - core)], text[half_rows(2 * c + core)]], axis=0
         ).astype(F32)
         squares = rows * rows
-        sums = squares[:, :128]
-        for g in range(1, feat // 128):
-            sums = sums + squares[:, g * 128 : (g + 1) * 128]
+        groups = [slice(g * 128, (g + 1) * 128) for g in range(feat // 128)]
+        sums = squares[:, groups[0]]
+        for group in groups[1:]:
+            sums = sums + squares[:, group]
         sq_away_out[slot] = sums[:rows_half]
         sq_half[c] = sums[rows_half:]
-        scaled = (rows * gain_ref[...].astype(F32)).astype(BF)
+        gain = gain_ref[...].astype(F32)
+        scaled = jnp.concatenate(
+            [(rows[:, group] * gain[g : g + 1]).astype(BF) for g, group in enumerate(groups)], axis=1
+        )
         tile = math.gcd(qwidth, 1024)
         for t in range(0, qwidth, tile):
             value = jnp.dot(scaled, wq[:, t : t + tile], preferred_element_type=F32)
-            away_out[slot, :, t : t + tile] = value[:rows_half].astype(BF)
+            for x in range(n_x):
+                att[outgoing(c) + x, :, t : t + tile] = value[x * sub : (x + 1) * sub].astype(BF)
             own_half[c % keep, :, t : t + tile] = value[rows_half:]
         for which in (0, 1):
             away(c, which).start()
@@ -244,14 +298,14 @@
 
         for j in range(1, n_x):
             rows = strip(other_x(j))
-            x_out[slot, j - 1] = (own_half[c % keep, rows] + away_in[c, rows].astype(F32)).astype(BF)
+            x_out[slot, j - 1] = (own_half[c % keep, rows] + away_in[c, other_x(j)].astype(F32)).astype(BF)
             sq_x_out[slot, j - 1] = sq_half[c, rows] + sq_away_in[c, rows]
             for which in (0, 1):
                 aside(c, j, which).start()
 
     def finish(c):
         rows = strip(x_me)
-        value = own_half[c % keep, rows] + away_in[c, rows].astype(F32)
+        value = own_half[c % keep, rows] + away_in[c, x_me].astype(F32)
         square = sq_half[c, rows] + sq_away_in[c, rows]
         for j in range(1, n_x):
             for which in (0, 1):
@@ -262,8 +316,13 @@
         query[...] = (value * lax.rsqrt(mean + 1e-05)).astype(BF)
 
     def attend(c):
-        img = img_ref[strip(c)]
-        allowed = img == own_ref[...]
+        line = jnp.broadcast_to(img_ref[pl.ds(c, 1)], (sub, rows_all)).astype(F32)
+        lane = lax.broadcasted_iota(jnp.int32, (sub, rows_all), 1)
+        token = lax.broadcasted_iota(jnp.int32, (sub, rows_all), 0) + own * sub
+        img = jnp.sum(jnp.where(lane == token, line, 0.0), axis=1, keepdims=True)
+        slot = lax.broadcasted_iota(jnp.int32, (1, n_seq * lat_rows), 1)
+        owner = lax.div(slot, jnp.int32(lat_count)).astype(F32)
+        allowed = img == owner
         visible = (img >= 0).astype(F32)
         cuts = [slice(h * HEAD, (h + 1) * HEAD) for h in range(heads)]
         logits = [
@@ -336,16 +395,14 @@
         def _():
             j = me // stride
             rows = page_rows(j)
-            value = part_ref[rows]
+            value = part_sum[rows]
             for k in range(1, n):
                 z = other_z(k)
                 remote(
                     part_ref.at[rows], lat_in.at[z], lat_send.at[0], lat_recv.at[z], tensor=z
                 ).wait_recv()
-                value = value + lat_in[z]
-            base = (j * part_rows) % lat_ref.shape[0]
-            mine = lat_ref[pl.ds(pl.multiple_of(base, part_rows), part_rows)].astype(F32)
-            pages[seq_me, rows] = (mine + value).astype(BF)
+                value = value + lat_in[z].astype(F32)
+            pages[seq_me, rows] = (lat_own[...].astype(F32) + value).astype(BF)
             for k in range(1, n):
                 page_piece(j, other_z(k), k - 1).start()
 
@@ -370,6 +427,9 @@
                 page_core(other_x(i), i, j).start()
 
     def keys_values():
+        for c in range(max(count - RING, 0), count):
+            for which in (0, 1):
+                away(c, which).wait_send()
         load_k.wait()
         load_v.wait()
         for x in range(n_x):
@@ -378,19 +438,16 @@
         rows = pages[...].reshape(n_seq * lat_rows, vis)
         tile = math.gcd(qwidth, 1024)
         for base, target in ((0, keys), (vis, values)):
-            @pl.loop(0, qwidth // tile)
-            def _(t, base=base, target=target):
-                cols = pl.ds(pl.multiple_of(t * tile, tile), tile)
-                target[:, cols] = jnp.dot(
-                    rows, wkv[base : base + vis, cols], preferred_element_type=F32
+            for t in range(0, qwidth, tile):
+                target[:, t : t + tile] = jnp.dot(
+                    rows, wkv[base : base + vis, t : t + tile], preferred_element_type=F32
                 ).astype(BF)
         if shared:
             load_o.start()
 
-    load_text(0).start()
-    load_q.start()
-    for c in range(1, min(SOON, count)):
-        load_text(c).start()
+    for load in (*load_res, load_own):
+        load.start()
+
     barrier = pltpu.get_barrier_semaphore()
 
     def greet(**where):
@@ -401,6 +458,13 @@
         greet(seq=2 * other_x(j) + core)
     for j in range(1, n):
         greet(tensor=other_z(j))
+    for load in (load_res[6], load_res[7], load_own):
+        load.wait()
+    load_text(0).start()
+    load_q.start()
+    for c in range(1, min(SOON, count)):
+        load_text(c).start()
+    resample()
     pl.semaphore_wait(barrier, 1 + (n_x - 1) + (n - 1))
 
     for j in range(owners):
@@ -505,7 +569,6 @@
 
     for c in range(max(count - RING, 0), count):
         for which in (0, 1):
-            away(c, which).wait_send()
             for j in range(1, n_x):
                 aside(c, j, which).wait_send()
     for k in range(owners):
@@ -524,11 +587,12 @@
             page_piece(me // stride, other_z(k), k - 1).wait_send()
 
 
-def flow(partial_value, latents, gain, img, owner, text, wq, wk, wv, wo, n_x, n):
+def flow(patches, latents, gain, text_image, wq_res, wk_res, wv_res, wo_res, text, wq, wk, wv, wo, n_x, n):
     n_seq = 2 * n_x
     tokens, feat = text.shape
     qwidth, width = wo.shape
-    lat_rows, vis = partial_value.shape
+    vis = patches.shape[1]
+    lat_rows = patches.shape[0] // PATCH_IMG * latents.shape[0]
     sub = math.gcd(tokens // n_seq, SUB)
     count = tokens // (n_seq * sub)
     blocks = count * n_seq
@@ -536,18 +600,39 @@
     owners = math.gcd(n, lat_rows // 16)
     shared = qwidth == width and qwidth <= 2 * vis
     tight = qwidth == width and tokens <= feat
+    roomy = tight and tokens + n_seq * (sub + lat_rows) + sub <= feat
     dma = pltpu.SemaphoreType.DMA
     vmem, anywhere = pl.BlockSpec(memory_space=pltpu.VMEM), pl.BlockSpec(memory_space=pltpu.HBM)
     others = max(n_x - 1, 1)
     half_rows = n_x * sub
-    stay = [pltpu.with_memory_space_constraint(v, pltpu.HBM) for v in (text, wq, wk, wv, wo)]
+    gain, img = gain.reshape(-1, 128), text_image.reshape(count, -1)
+    res = wo_res.shape[0]
+    windowed = (
+        res % 128 == 0 and 3 * res <= qwidth and vis <= qwidth and res + latents.shape[0] <= vis
+    )
+    stay = [
+        pltpu.with_memory_space_constraint(value, pltpu.HBM)
+        for value in (
+            patches, latents, gain, img, wq_res, wk_res, wv_res, wo_res, text, wq, wk, wv, wo
+        )
+    ]
     scratch = [
+        ((lat_rows, vis), F32),
+        ((lat_rows, vis), BF),
+        ((16, 128) if windowed else latents.shape, BF),
+        ((lat_rows // owners, vis), BF),
+        (gain.shape, BF),
+        (img.shape, jnp.int32),
+        (patches.shape, BF),
+        *(
+            ((16, 128) if windowed else value.shape, BF)
+            for value in (wq_res, wk_res, wv_res, wo_res)
+        ),
         ((feat, qwidth), BF),
         ((2 * vis, qwidth), BF),
         ((16, 128) if shared else (qwidth, width), BF),
         ((min(count, LEAD + 2), half_rows, qwidth), F32),
-        ((RING, half_rows, qwidth), BF),
-        ((count, half_rows, qwidth), BF),
+        ((count, n_x, sub, qwidth), BF),
         ((RING, others, sub, qwidth), BF),
         ((count, others, sub, qwidth), BF),
         ((count, half_rows, 128), F32),
@@ -555,28 +640,29 @@
         ((count, half_rows, 128), F32),
         ((RING, others, sub, 128), F32),
         ((count, others, sub, 128), F32),
-        ((sub, qwidth), BF),
-        ((n_seq * lat_rows, qwidth), BF),
+        ((16, 128) if roomy else (sub, qwidth), BF),
+        ((16, 128) if roomy else (n_seq * lat_rows, qwidth), BF),
         ((n_seq * lat_rows, qwidth), BF),
         ((n_seq, lat_rows, vis), BF),
-        ((n, lat_rows // owners, vis), F32),
+        ((n, lat_rows // owners, vis), BF),
         ((blocks, sub, qwidth), BF),
         ((1, 16, 128) if shared else (blocks, sub, width), BF),
         ((16, 128) if tight else (tokens, width), BF),
-        ((n_seq * sub, width), BF),
+        ((16, 128) if roomy else (n_seq * sub, width), BF),
     ]
     return pl.pallas_call(
-        functools.partial(flow_kernel, (n_x, n, count, sub, owners, shared, tight)),
+        functools.partial(flow_kernel, (n_x, n, count, sub, owners, shared, tight, roomy, windowed)),
         out_shape=(
             jax.ShapeDtypeStruct((tokens, width), BF),
             jax.ShapeDtypeStruct((tokens, feat), BF),
             jax.ShapeDtypeStruct((lat_rows, vis), BF),
         ),
-        in_specs=[vmem] * 5 + [anywhere] * 5,
+        in_specs=[anywhere] * len(stay),
         out_specs=(vmem, vmem, vmem),
         scratch_shapes=[pltpu.VMEM(shape, kind) for shape, kind in scratch]
         + [
             dma((4,)),
+            dma((9,)),
             dma((count,)),
             dma((2, RING)),
             dma((2, count)),
@@ -599,7 +685,7 @@
             collective_id=0, has_side_effects=True, vmem_limit_bytes=41984 << 10
         ),
         name="flow",
-    )(partial_value, latents, gain, img, owner, *stay)
+    )(*stay)
 
 
 def close_kernel(rows, slots, text_ref, gate_ref, branch_ref, page_ref, out_ref, page_out, buf, sem, page_sem):
@@ -673,18 +759,8 @@
         gate_x,
         text_image,
     ):
-        seq_me = lax.axis_index("seq")
-        block = (seq_me % 2) * n_x + seq_me // 2
-        lat_count = latents.shape[0]
-        tokens = text.shape[0]
-        sub = math.gcd(tokens // n_seq, SUB)
-        img = lax.dynamic_index_in_dim(
-            text_image.reshape(-1, n_seq, sub), block, 1, keepdims=False
-        ).reshape(-1, 1)
-        partial_value = resample(patches, latents, wq_res, wk_res, wv_res, wo_res)
-        owner = jnp.arange(n_seq * partial_value.shape[0], dtype=jnp.int32) // lat_count
         branch, text, page_latents = flow(
-            partial_value, latents, norm_gain[None, :], img, owner[None, :], text,
+            patches, latents, norm_gain, text_image, wq_res, wk_res, wv_res, wo_res, text,
             wq_x, wk_x, wv_x, wo_x, n_x, n_tensor,
         )
         return close(text, gate_x[None, :], branch, page_latents)

time: 203 us -> 196 us (0.966)
  matrix products: 5.96 us -> 0 us
  local copies, waits for them, and re-layouts: 2.76 us -> 0.01 us
    dot_general x6 -> x0, matrix products: 5.96 us -> none  [the longest x1 1.92 us: resample(): jnp.dot(patches, wv_res, preferred_element_type=F32).astype(BF)]
    pallas_call x1, Pallas kernels: 188 us -> 190 us  [flow(): pl.pallas_call(functools.partial(flow_kernel, (n_x, n, count, sub, owners...]
where the time goes in v3:
time: 196 us
  Pallas kernels  195 us (99%)
    pallas_call x1, Pallas kernels, flow(): pl.pallas_call(functools.partial(flow_kernel, (n_x, n, count, sub, owners...  190 us
    pallas_call x1, Pallas kernels, close(): pl.pallas_call(functools.partial(close_kernel, rows, slots), out_shape=(j...  4.7 us

profile of v3, /device:TPU:0, one launch (start us, length us, event | category | flops | bytes accessed | tf_op | source)
XLA Modules:
  0.0 195.8 jit_solution(13973140267683535349)
XLA Ops:
  0.6 0.0 copy-start
  0.6 190.5 %flow.1 = (bf16[1536,2048]{1,0:T(8,128)(2,1)S(1)}, bf16[1536,2048]{1,0:T(8,128)(2,1)S(1)}, bf16[64,1280]{1,0:T(8,128)(2,1)S(1)}) custom-call(bf16[257,1280]{1,0:T(8,128)(2,1)} %refs_0_.1, bf16[64,1280]{1,0:T(8,128)(2,1)} %refs_1_.1, bf16[16,128]{1,0:T(8,128)(2,1)} %bitcast.5, s32[12,128]{1,0:T(8,128)} %bitcast.4, bf16[1280,384]{1,0:T(8,128)(2,1)} %refs_4_.1, ...), custom_call_target="tpu_custom_call" | custom-call | tf_op jit(solution)/shard_map/flow/pallas_call | solution.py:653
  191.1 0.0 copy-done
  191.1 4.7 %close.1 = (f32[1536,2048]{1,0:T(8,128)}, bf16[64,1280]{1,0:T(8,128)(2,1)}) custom-call(bf16[1536,2048]{1,0:T(8,128)(2,1)S(1)} %get-tuple-element.5.text_ref, f32[1,2048]{1,0:T(1,128)S(1)} %bitcast.3, bf16[1536,2048]{1,0:T(8,128)(2,1)S(1)} %get-tuple-element.6.branch_ref, bf16[64,1280]{1,0:T(8,128)(2,1)S(1)} %get-tuple-element.7.page_ref), custom_call_target="tpu_custom_call" | custom-call | tf_op jit(solution)/shard_map/close/pallas_call | solution.py:725
Async XLA Ops:
  0.6 190.5 %copy-start = (f32[2048]{0:T(1024)S(1)}, f32[2048]{0:T(1024)}, u32[]{:S(2)}) copy-start(f32[2048]{0:T(1024)} %param.26) | copy-start | bytes 24580

commit v4 on v3

--- a/solution.py
+++ b/solution.py
@@ -15,10 +15,10 @@
 CUT = 2
 TILES = 2
 SOON = 2
-LAG = 3
-LEAD = 12
-SUM_STEP, PAGE_STEP, PASS_STEP = 4, 7, 10
-EARLY, AHEAD, LATER = 2, 2, 11
+LAG, SHORT = 4, 2
+LEAD = 10
+SUM_STEP, PAGE_STEP, PASS_STEP = 3, 6, 9
+EARLY, AHEAD, LATER = 1, 2, 9
 RING = 2
 BF = jnp.bfloat16
 F32 = jnp.float32
@@ -58,10 +58,9 @@
     stride = n // owners
     wo = wkv if shared else late
     if roomy:
-        at = count * rows_all
-        mixed_rows = wq.at[pl.ds(at, rows_all)]
-        keys = wq.at[pl.ds(at + rows_all, n_seq * lat_rows)]
-        query = wq.at[pl.ds(at + rows_all + n_seq * lat_rows, sub)]
+        keys = wkv.at[pl.ds(qwidth, n_seq * lat_rows)]
+        mixed_rows = wkv.at[pl.ds(qwidth + n_seq * lat_rows, rows_all)]
+        query = wkv.at[pl.ds(qwidth + n_seq * lat_rows + rows_all, sub)]
     part = att if shared else second
 
     def remote(src, dst, sent, got, **where):
@@ -427,9 +426,6 @@
                 page_core(other_x(i), i, j).start()
 
     def keys_values():
-        for c in range(max(count - RING, 0), count):
-            for which in (0, 1):
-                away(c, which).wait_send()
         load_k.wait()
         load_v.wait()
         for x in range(n_x):
@@ -437,7 +433,7 @@
                 page_from_core(x, k).wait_recv()
         rows = pages[...].reshape(n_seq * lat_rows, vis)
         tile = math.gcd(qwidth, 1024)
-        for base, target in ((0, keys), (vis, values)):
+        for base, target in ((vis, values), (0, keys)):
             for t in range(0, qwidth, tile):
                 target[:, t : t + tile] = jnp.dot(
                     rows, wkv[base : base + vis, t : t + tile], preferred_element_type=F32
@@ -486,17 +482,9 @@
         pl.when(s == PAGE_STEP)(share_page)
         pl.when(s == PASS_STEP)(pass_pages)
 
-        @pl.when(s < count)
+        @pl.when(s < min(count, LEAD))
         def _():
             project(s)
-
-            if tight:
-                @pl.when(jnp.logical_and(s == count - 1, depth > 0))
-                def _():
-                    pl.semaphore_signal(
-                        free_sem, inc=1, device_id={"tensor": outer},
-                        device_id_type=pl.DeviceIdType.MESH,
-                    )
 
         @pl.when(jnp.logical_and(s >= EARLY, s < EARLY + min(AHEAD, count)))
         def _():
@@ -513,7 +501,15 @@
                     p = (c - 1) * per + b
                     gather(p)
 
-                    @pl.when(jnp.logical_and(depth > 0, p >= lag))
+                    @pl.when(
+                        jnp.logical_and(depth > 0, jnp.logical_and(p < per, p >= lag - SHORT))
+                    )
+                    def _():
+                        spread(p - lag + SHORT)
+
+                    @pl.when(
+                        jnp.logical_and(depth > 0, jnp.logical_and(p >= per + SHORT, p >= lag))
+                    )
                     def _():
                         spread(p - lag)
 
@@ -535,6 +531,23 @@
         @pl.when(jnp.logical_and(s >= LATER + AHEAD, s < LATER + count))
         def _():
             scatter(s - LATER)
+
+        @pl.when(s == LEAD)
+        def _():
+            @pl.loop(LEAD, count)
+            def _(later):
+                project(later)
+
+            for last in range(max(count - RING, 0), count):
+                for which in (0, 1):
+                    away(last, which).wait_send()
+            if tight:
+                @pl.when(depth > 0)
+                def _():
+                    pl.semaphore_signal(
+                        free_sem, inc=1, device_id={"tensor": outer},
+                        device_id_type=pl.DeviceIdType.MESH,
+                    )
 
         pl.when(c == 0)(load_o.wait)
         pieces(per // 2, 3 * per // 4)
@@ -600,7 +613,7 @@
     owners = math.gcd(n, lat_rows // 16)
     shared = qwidth == width and qwidth <= 2 * vis
     tight = qwidth == width and tokens <= feat
-    roomy = tight and tokens + n_seq * (sub + lat_rows) + sub <= feat
+    roomy = shared and vis <= qwidth and qwidth + n_seq * (sub + lat_rows) + sub <= 2 * vis
     dma = pltpu.SemaphoreType.DMA
     vmem, anywhere = pl.BlockSpec(memory_space=pltpu.VMEM), pl.BlockSpec(memory_space=pltpu.HBM)
     others = max(n_x - 1, 1)

time: 196 us -> 193 us (0.985)
  Pallas kernels: 195 us -> 193 us
    pallas_call x1, Pallas kernels: 190 us -> 188 us  [flow(): pl.pallas_call(functools.partial(flow_kernel, (n_x, n, count, sub, owners...]
where the time goes in v4:
time: 193 us
  Pallas kernels  193 us (100%)
    pallas_call x1, Pallas kernels, flow(): pl.pallas_call(functools.partial(flow_kernel, (n_x, n, count, sub, owners...  188 us
    pallas_call x1, Pallas kernels, close(): pl.pallas_call(functools.partial(close_kernel, rows, slots), out_shape=(j...  4.7 us

profile of v4, /device:TPU:0, one launch (start us, length us, event | category | flops | bytes accessed | tf_op | source)
XLA Modules:
  0.0 193.3 jit_solution(3821677740443544862)
XLA Ops:
  0.6 0.0 copy-start
  0.6 187.9 %flow.1 = (bf16[1536,2048]{1,0:T(8,128)(2,1)S(1)}, bf16[1536,2048]{1,0:T(8,128)(2,1)S(1)}, bf16[64,1280]{1,0:T(8,128)(2,1)S(1)}) custom-call(bf16[257,1280]{1,0:T(8,128)(2,1)} %refs_0_.1, bf16[64,1280]{1,0:T(8,128)(2,1)} %refs_1_.1, bf16[16,128]{1,0:T(8,128)(2,1)} %bitcast.5, s32[12,128]{1,0:T(8,128)} %bitcast.4, bf16[1280,384]{1,0:T(8,128)(2,1)} %refs_4_.1, ...), custom_call_target="tpu_custom_call" | custom-call | tf_op jit(solution)/shard_map/flow/pallas_call | solution.py:666
  188.6 0.0 copy-done
  188.6 4.7 %close.1 = (f32[1536,2048]{1,0:T(8,128)}, bf16[64,1280]{1,0:T(8,128)(2,1)}) custom-call(bf16[1536,2048]{1,0:T(8,128)(2,1)S(1)} %get-tuple-element.5.text_ref, f32[1,2048]{1,0:T(1,128)S(1)} %bitcast.3, bf16[1536,2048]{1,0:T(8,128)(2,1)S(1)} %get-tuple-element.6.branch_ref, bf16[64,1280]{1,0:T(8,128)(2,1)S(1)} %get-tuple-element.7.page_ref), custom_call_target="tpu_custom_call" | custom-call | tf_op jit(solution)/shard_map/close/pallas_call | solution.py:738
Async XLA Ops:
  0.6 187.9 %copy-start = (f32[2048]{0:T(1024)S(1)}, f32[2048]{0:T(1024)}, u32[]{:S(2)}) copy-start(f32[2048]{0:T(1024)} %param.26) | copy-start | bytes 24580

commit v5 on v4

--- a/solution.py
+++ b/solution.py
@@ -225,11 +225,18 @@
         ref = att.at[c * n_seq + core * n_x + x]
         return remote(ref, ref, block_sem.at[c, n_x + j - 1], side_sem.at[c, x], seq=2 * x + core)
 
+    def block_at(c, q):
+        return c * n_seq + (q % 2) * n_x + (x_me + q // 2) % n_x
+
+    def spot(p):
+        block = p // cut
+        return block_at(block // n_seq, block % n_seq)
+
     def rows_of(p):
-        return pl.ds(pl.multiple_of(p * size, size), size)
+        return pl.ds(pl.multiple_of(spot(p) * sub + (p % cut) * size, size), size)
 
     def piece(p):
-        return part.at[p // cut, pl.ds(pl.multiple_of((p % cut) * size, size), size)]
+        return part.at[spot(p), pl.ds(pl.multiple_of((p % cut) * size, size), size)]
 
     def landing(p):
         return (wq if tight else came).at[rows_of(p)]
@@ -343,20 +350,23 @@
             to_x(c, j).start()
         to_core(c, x_me, 0).start()
 
-    def product(c, t):
+    def product(c, t, low, high):
         tile = width // TILES
         cols = slice(t * tile, (t + 1) * tile)
-        rows = att[pl.ds(c * n_seq, n_seq)].reshape(rows_all, qwidth)
+        rows = jnp.concatenate([att[block_at(c, q)] for q in range(low, high)], axis=0)
         value = jnp.dot(rows, wo[:qwidth, cols], preferred_element_type=F32)
-        mixed_rows[:, cols] = value.astype(BF)
-
-    def replace(c):
-        for j in range(n_x):
-            to_core(c, x_me, j).wait_send()
-        for j in range(1, n_x):
-            to_x(c, j).wait_send()
-        for b in range(n_seq):
-            part[c * n_seq + b] = mixed_rows[b * sub : (b + 1) * sub]
+        mixed_rows[low * sub : high * sub, cols] = value.astype(BF)
+
+    def replace(c, low, high):
+        if low == 0:
+            to_core(c, x_me, 0).wait_send()
+            for j in range(1, n_x):
+                to_x(c, j).wait_send()
+        if high == n_seq:
+            for j in range(1, n_x):
+                to_core(c, x_me, j).wait_send()
+        for q in range(low, high):
+            part[block_at(c, q)] = mixed_rows[q * sub : (q + 1) * sub]
 
     def gather(p):
         @pl.when(depth > 0)
@@ -499,7 +509,10 @@
                 @pl.loop(low, high)
                 def _(b):
                     p = (c - 1) * per + b
-                    gather(p)
+
+                    @pl.when(jnp.logical_or(depth > 0, p >= 2 * cut))
+                    def _():
+                        gather(p)
 
                     @pl.when(
                         jnp.logical_and(depth > 0, jnp.logical_and(p < per, p >= lag - SHORT))
@@ -549,22 +562,51 @@
                         device_id_type=pl.DeviceIdType.MESH,
                     )
 
-        pl.when(c == 0)(load_o.wait)
+        @pl.when(s == LEAD)
+        def _():
+            load_o.wait()
+            from_core(0, x_me).wait_recv()
+            for t in range(TILES):
+                product(0, t, 0, 2)
+            replace(0, 0, 2)
+
+            @pl.when(depth == 0)
+            def _():
+                @pl.loop(0, 2 * cut)
+                def _(p):
+                    gather(p)
+
         pieces(per // 2, 3 * per // 4)
 
         @pl.when(ready)
         def _():
-            for x in range(n_x):
-                from_core(c, x).wait_recv()
-            product(c, 0)
+            for j in range(1, n_x):
+                from_core(c, other_x(j)).wait_recv()
+
+            @pl.when(c >= 1)
+            def _():
+                from_core(c, x_me).wait_recv()
+                product(c, 0, 0, n_seq)
+
+            @pl.when(c == 0)
+            def _():
+                product(0, 0, 2, n_seq)
 
         pieces(3 * per // 4, per)
 
         @pl.when(ready)
         def _():
-            for t in range(1, TILES):
-                product(c, t)
-            replace(c)
+            @pl.when(c >= 1)
+            def _():
+                for t in range(1, TILES):
+                    product(c, t, 0, n_seq)
+                replace(c, 0, n_seq)
+
+            @pl.when(c == 0)
+            def _():
+                for t in range(1, TILES):
+                    product(0, t, 2, n_seq)
+                replace(0, 2, n_seq)
 
     @pl.loop(0, total)
     def _(p):

time: 193 us -> 196 us (1.016)
  Pallas kernels: 193 us -> 195 us
    pallas_call x1, Pallas kernels: 188 us -> 190 us  [flow(): pl.pallas_call(functools.partial(flow_kernel, (n_x, n, count, sub, owners...]
where the time goes in v5:
time: 196 us; the launch traced here: 195 us
  Pallas kernels  195 us (99%)
    pallas_call x1, Pallas kernels, flow(): pl.pallas_call(functools.partial(flow_kernel, (n_x, n, count, sub, owners...  190 us
    pallas_call x1, Pallas kernels, close(): pl.pallas_call(functools.partial(close_kernel, rows, slots), out_shape=(j...  4.7 us

profile of v5, /device:TPU:0, one launch (start us, length us, event | category | flops | bytes accessed | tf_op | source)
XLA Modules:
  0.0 195.4 jit_solution(9426427762945879498)
XLA Ops:
  0.6 0.0 copy-start
  0.6 190.0 %flow.1 = (bf16[1536,2048]{1,0:T(8,128)(2,1)S(1)}, bf16[1536,2048]{1,0:T(8,128)(2,1)S(1)}, bf16[64,1280]{1,0:T(8,128)(2,1)S(1)}) custom-call(bf16[257,1280]{1,0:T(8,128)(2,1)} %refs_0_.1, bf16[64,1280]{1,0:T(8,128)(2,1)} %refs_1_.1, bf16[16,128]{1,0:T(8,128)(2,1)} %bitcast.5, s32[12,128]{1,0:T(8,128)} %bitcast.4, bf16[1280,384]{1,0:T(8,128)(2,1)} %refs_4_.1, ...), custom_call_target="tpu_custom_call" | custom-call | tf_op jit(solution)/shard_map/flow/pallas_call | solution.py:708
  190.7 0.0 copy-done
  190.7 4.7 %close.1 = (f32[1536,2048]{1,0:T(8,128)}, bf16[64,1280]{1,0:T(8,128)(2,1)}) custom-call(bf16[1536,2048]{1,0:T(8,128)(2,1)S(1)} %get-tuple-element.5.text_ref, f32[1,2048]{1,0:T(1,128)S(1)} %bitcast.3, bf16[1536,2048]{1,0:T(8,128)(2,1)S(1)} %get-tuple-element.6.branch_ref, bf16[64,1280]{1,0:T(8,128)(2,1)S(1)} %get-tuple-element.7.page_ref), custom_call_target="tpu_custom_call" | custom-call | tf_op jit(solution)/shard_map/close/pallas_call | solution.py:780
Async XLA Ops:
  0.6 190.1 %copy-start = (f32[2048]{0:T(1024)S(1)}, f32[2048]{0:T(1024)}, u32[]{:S(2)}) copy-start(f32[2048]{0:T(1024)} %param.26) | copy-start | bytes 24580

commit v6 on v4

--- a/solution.py
+++ b/solution.py
@@ -16,9 +16,9 @@
 TILES = 2
 SOON = 2
 LAG, SHORT = 4, 2
-LEAD = 10
-SUM_STEP, PAGE_STEP, PASS_STEP = 3, 6, 9
-EARLY, AHEAD, LATER = 1, 2, 9
+LEAD = 9
+SUM_STEP, PAGE_STEP, PASS_STEP = 3, 6, 8
+EARLY, AHEAD, LATER = 1, 2, 8
 RING = 2
 BF = jnp.bfloat16
 F32 = jnp.float32

time: 193 us -> 193 us (level)
  no operation moved by 1% of the time
where the time goes in v6:
time: 193 us
  Pallas kernels  192 us (99%)
    pallas_call x1, Pallas kernels, flow(): pl.pallas_call(functools.partial(flow_kernel, (n_x, n, count, sub, owners...  188 us
    pallas_call x1, Pallas kernels, close(): pl.pallas_call(functools.partial(close_kernel, rows, slots), out_shape=(j...  4.7 us

profile of v6, /device:TPU:0, one launch (start us, length us, event | category | flops | bytes accessed | tf_op | source)
XLA Modules:
  0.0 193.1 jit_solution(8043440106795758590)
XLA Ops:
  0.6 0.0 copy-start
  0.6 187.8 %flow.1 = (bf16[1536,2048]{1,0:T(8,128)(2,1)S(1)}, bf16[1536,2048]{1,0:T(8,128)(2,1)S(1)}, bf16[64,1280]{1,0:T(8,128)(2,1)S(1)}) custom-call(bf16[257,1280]{1,0:T(8,128)(2,1)} %refs_0_.1, bf16[64,1280]{1,0:T(8,128)(2,1)} %refs_1_.1, bf16[16,128]{1,0:T(8,128)(2,1)} %bitcast.5, s32[12,128]{1,0:T(8,128)} %bitcast.4, bf16[1280,384]{1,0:T(8,128)(2,1)} %refs_4_.1, ...), custom_call_target="tpu_custom_call" | custom-call | tf_op jit(solution)/shard_map/flow/pallas_call | solution.py:666
  188.4 0.0 copy-done
  188.4 4.7 %close.1 = (f32[1536,2048]{1,0:T(8,128)}, bf16[64,1280]{1,0:T(8,128)(2,1)}) custom-call(bf16[1536,2048]{1,0:T(8,128)(2,1)S(1)} %get-tuple-element.5.text_ref, f32[1,2048]{1,0:T(1,128)S(1)} %bitcast.3, bf16[1536,2048]{1,0:T(8,128)(2,1)S(1)} %get-tuple-element.6.branch_ref, bf16[64,1280]{1,0:T(8,128)(2,1)S(1)} %get-tuple-element.7.page_ref), custom_call_target="tpu_custom_call" | custom-call | tf_op jit(solution)/shard_map/close/pallas_call | solution.py:738
Async XLA Ops:
  0.6 187.8 %copy-start = (f32[2048]{0:T(1024)S(1)}, f32[2048]{0:T(1024)}, u32[]{:S(2)}) copy-start(f32[2048]{0:T(1024)} %param.26) | copy-start | bytes 24580
